TPU v7x, 32 devices: a whole 2x2x4 slice. The times are simulated.
32 devices in a mesh: dp: 8 (over z, y), mp: 4 (over x, core).
Axes of the slice: x: 2, y: 2, z: 4, core: 2. Of those that a mesh axis runs over, the one named last changes fastest.
Arguments:
- tokens: bfloat16 [24576, 768], P('dp'), may hold values from -6 to 6
- out_grad: bfloat16 [24576, 768], P('dp'), may hold values from -6 to 6
- pair_start: int32 [48, 12], P('dp'), may hold values from 0 to 471, as said below
- caption_len: int32 [48, 12], P('dp'), may hold values from 0 to 60, as said below
- region_len: int32 [48, 12], P('dp'), may hold values from 0 to 100, as said below
- w_query: bfloat16 [768, 768], P(None, 'mp'), may hold values from -0.21875 to 0.21875
- w_key: bfloat16 [768, 768], P(None, 'mp'), may hold values from -0.21875 to 0.21875
- w_value: bfloat16 [768, 768], P(None, 'mp'), may hold values from -0.21875 to 0.21875
- b_query: float32 [768], P('mp'), may hold values from -3 to 3
- b_value: float32 [768], P('mp'), may hold values from -3 to 3
- w_out: bfloat16 [768, 768], P('mp'), may hold values from -1.25 to 1.25
- b_out: float32 [768], replicated, may hold values from -2 to 2
- mixed_gain: float32 [768], replicated, may hold values from 0.5 to 1.5
- mixed_shift: float32 [768], replicated, may hold values from -2 to 2
- w_up: bfloat16 [768, 3072], P(None, 'mp'), may hold values from -0.21875 to 0.21875
- b_up: float32 [3072], P('mp'), may hold values from -3 to 3
- w_down: bfloat16 [3072, 768], P('mp'), may hold values from -0.109375 to 0.109375
- b_down: float32 [768], replicated, may hold values from -2 to 2
- final_gain: float32 [768], replicated, may hold values from 0.5 to 1.5
- final_shift: float32 [768], replicated, may hold values from -2 to 2
Outputs:
- layer_out: bfloat16 [24576, 768], P(('dp', 'mp'))
- tokens_grad: bfloat16 [24576, 768], P(('dp', 'mp'))
- w_query_grad: float32 [768, 768], P('dp', 'mp')
- w_key_grad: float32 [768, 768], P('dp', 'mp')
- w_value_grad: float32 [768, 768], P('dp', 'mp')
- b_query_grad: float32 [768], P(('mp', 'dp'))
- b_value_grad: float32 [768], P(('mp', 'dp'))
- w_out_grad: float32 [768, 768], P('mp', 'dp')
- b_out_grad: float32 [768], P('dp')
- mixed_gain_grad: float32 [768], P(('dp', 'mp'))
- mixed_shift_grad: float32 [768], P(('dp', 'mp'))
- w_up_grad: float32 [768, 3072], P('dp', 'mp')
- b_up_grad: float32 [3072], P(('mp', 'dp'))
- w_down_grad: float32 [3072, 768], P('mp', 'dp')
- b_down_grad: float32 [768], P('dp')
- final_gain_grad: float32 [768], P(('dp', 'mp'))
- final_shift_grad: float32 [768], P(('dp', 'mp'))
Inputs may be any that keep to these rules, and one draw needn't show every extreme that they name: In each packed block the used slots come first; a used slot starts where the one before it ends (the first at 0), holds caption_len of 5 to 60 and region_len of 36 to 100, and all used pairs end by 512; unused slots have pair_start 0. `caption_len`: 0 marks an unused slot; some block holds a pair of 60 caption words. `region_len`: 0 marks an unused slot; some pair with 60 caption words has 100 regions.
All inputs are finite; a program needn't handle non-finite values.
Results may differ from a plain program's by a relative error of at most 0.03.
Values may be sent and summed in bfloat16 or wider, within the bound.
A program may use at most 256 MiB of HBM per device.

v0:
```python
import jax
import jax.numpy as jnp
from jax import lax
from jax.sharding import PartitionSpec as P

HD = 64
BIN = 512
SLOTS = 12


epsilon = 1e-05
negative = -1e30
root_half = 0.7071067811865476
density_factor = 0.3989422804014327


def pair_ids(pair_start, caption_len, region_len):
    places = jnp.arange(BIN, dtype=jnp.int32)
    finish = pair_start + caption_len + region_len
    inside = (places[None, :, None] >= pair_start[:, None, :]) & (
        places[None, :, None] < finish[:, None, :]
    )
    numbers = jnp.arange(1, SLOTS + 1, dtype=jnp.int32)
    return jnp.max(jnp.where(inside, numbers, 0), axis=2)


def layer_norm(value, norm_gain, norm_shift):
    centered = value - jnp.mean(value, axis=-1, keepdims=True)
    inverse = lax.rsqrt(jnp.mean(centered * centered, axis=-1, keepdims=True) + epsilon)
    normal = centered * inverse
    return (normal * norm_gain + norm_shift, normal, inverse)


def norm_back(upstream, normal, inverse, norm_gain):
    scaled = upstream * norm_gain
    return inverse * (
        scaled
        - jnp.mean(scaled, axis=-1, keepdims=True)
        - normal * jnp.mean(scaled * normal, axis=-1, keepdims=True)
    )


def gelu_slope(inner):
    return (
        0.5 * (1.0 + lax.erf(inner * root_half))
        + inner * jnp.exp(-0.5 * inner * inner) * density_factor
    )


def outer_sum(left, right):
    return lax.dot_general(
        left, right, (((0,), (0,)), ((), ())), preferred_element_type=jnp.float32
    )


def back_product(gradient, weight):
    return lax.dot_general(
        gradient, weight, (((1,), (1,)), ((), ())), preferred_element_type=jnp.float32
    )


def block_scores(queries, keys, labels):
    scores = jnp.einsum("qhd,khd->hqk", queries, keys, preferred_element_type=jnp.float32) * HD ** (
        -0.5
    )
    allowed = labels[:, None] == labels[None, :]
    return jnp.where(allowed[None], scores, negative)


def attend_forward(items):
    queries, keys, values, labels = items
    scores = block_scores(queries, keys, labels)
    highest = jnp.max(scores, axis=-1, keepdims=True)
    expo = jnp.exp(scores - highest)
    summed = jnp.sum(expo, axis=-1, keepdims=True)
    weights = (expo / summed).astype(jnp.bfloat16)
    mixed = jnp.einsum("hqk,khd->qhd", weights, values, preferred_element_type=jnp.float32)
    return (mixed, (highest + jnp.log(summed))[..., 0])


def attend_backward(items):
    queries, keys, values, labels, log_total, mixed_grad = items
    scores = block_scores(queries, keys, labels)
    weights = jnp.exp(scores - log_total[..., None])
    weight_grad = jnp.einsum("qhd,khd->hqk", mixed_grad, values, preferred_element_type=jnp.float32)
    centre = jnp.sum(weights * weight_grad, axis=-1, keepdims=True)
    score_grad = (weights * (weight_grad - centre)).astype(jnp.bfloat16)
    query_grad = jnp.einsum(
        "hqk,khd->qhd", score_grad, keys, preferred_element_type=jnp.float32
    ) * HD ** (-0.5)
    key_grad = jnp.einsum(
        "hqk,qhd->khd", score_grad, queries, preferred_element_type=jnp.float32
    ) * HD ** (-0.5)
    value_grad = jnp.einsum(
        "hqk,qhd->khd", weights.astype(jnp.bfloat16), mixed_grad, preferred_element_type=jnp.float32
    )
    return (
        query_grad.astype(jnp.bfloat16),
        key_grad.astype(jnp.bfloat16),
        value_grad.astype(jnp.bfloat16),
    )


def body(
    tokens,
    out_grad,
    pair_start,
    caption_len,
    region_len,
    w_query,
    w_key,
    w_value,
    b_query,
    b_value,
    w_out,
    b_out,
    mixed_gain,
    mixed_shift,
    w_up,
    b_up,
    w_down,
    b_down,
    final_gain,
    final_shift,
):
    count = tokens.shape[0]
    share = count // lax.axis_size("mp")
    offset = lax.axis_index("mp") * share
    local_width = w_query.shape[1]
    heads_local = local_width // HD
    blocks = count // BIN
    labels = pair_ids(pair_start, caption_len, region_len)
    valid = (labels.reshape(count) > 0).astype(jnp.float32)
    joined = jnp.concatenate([w_query, w_key, w_value], axis=1)
    projected = jnp.dot(tokens, joined, preferred_element_type=jnp.float32)
    queries = (projected[:, :local_width] + b_query).astype(jnp.bfloat16)
    keys = projected[:, local_width : 2 * local_width].astype(jnp.bfloat16)
    values = (projected[:, 2 * local_width :] + b_value).astype(jnp.bfloat16)
    shaped = (blocks, BIN, heads_local, HD)
    query_blocks = queries.reshape(shaped)
    key_blocks = keys.reshape(shaped)
    value_blocks = values.reshape(shaped)
    mixed, log_totals = lax.map(attend_forward, (query_blocks, key_blocks, value_blocks, labels))
    mixed_rows = mixed.reshape(count, local_width).astype(jnp.bfloat16)
    attention_part = jnp.dot(mixed_rows, w_out, preferred_element_type=jnp.float32).astype(
        jnp.bfloat16
    )
    first = tokens.astype(jnp.float32) + lax.psum(attention_part, "mp").astype(jnp.float32) + b_out
    normed, first_normal, first_inverse = layer_norm(first, mixed_gain, mixed_shift)
    normed_low = normed.astype(jnp.bfloat16)
    inner = jnp.dot(normed_low, w_up, preferred_element_type=jnp.float32) + b_up
    hidden = jax.nn.gelu(inner, approximate=False).astype(jnp.bfloat16)
    down_part = jnp.dot(hidden, w_down, preferred_element_type=jnp.float32).astype(jnp.bfloat16)
    second = normed + lax.psum(down_part, "mp").astype(jnp.float32) + b_down
    result, second_normal, second_inverse = layer_norm(second, final_gain, final_shift)
    layer_out = lax.dynamic_slice_in_dim(result, offset, share, 0).astype(jnp.bfloat16)
    upstream = out_grad.astype(jnp.float32) * valid[:, None]
    second_grad = norm_back(upstream, second_normal, second_inverse, final_gain)
    fed_grad = second_grad.astype(jnp.bfloat16)
    final_upstream = lax.dynamic_slice_in_dim(upstream, offset, share, 0)
    final_normal = lax.dynamic_slice_in_dim(second_normal, offset, share, 0)
    final_gain_grad = jnp.sum(final_upstream * final_normal, axis=0)
    final_shift_grad = jnp.sum(final_upstream, axis=0)
    b_down_grad = jnp.sum(fed_grad.astype(jnp.float32), axis=0)
    w_down_grad = outer_sum(hidden, fed_grad)
    inner_grad = (back_product(fed_grad, w_down) * gelu_slope(inner)).astype(jnp.bfloat16)
    b_up_grad = jnp.sum(inner_grad.astype(jnp.float32), axis=0)
    w_up_grad = outer_sum(normed_low, inner_grad)
    normed_part = back_product(inner_grad, w_up).astype(jnp.bfloat16)
    normed_grad = second_grad + lax.psum(normed_part, "mp").astype(jnp.float32)
    first_grad = norm_back(normed_grad, first_normal, first_inverse, mixed_gain)
    attended_grad = first_grad.astype(jnp.bfloat16)
    mixed_upstream = lax.dynamic_slice_in_dim(normed_grad, offset, share, 0)
    mixed_normal = lax.dynamic_slice_in_dim(first_normal, offset, share, 0)
    mixed_gain_grad = jnp.sum(mixed_upstream * mixed_normal, axis=0)
    mixed_shift_grad = jnp.sum(mixed_upstream, axis=0)
    b_out_grad = jnp.sum(attended_grad.astype(jnp.float32), axis=0)
    w_out_grad = outer_sum(mixed_rows, attended_grad)
    mixed_grad = back_product(attended_grad, w_out).astype(jnp.bfloat16)
    query_grad, key_grad, value_grad = lax.map(
        attend_backward,
        (query_blocks, key_blocks, value_blocks, labels, log_totals, mixed_grad.reshape(shaped)),
    )
    joined_grad = jnp.concatenate(
        [
            query_grad.reshape(count, local_width),
            key_grad.reshape(count, local_width),
            value_grad.reshape(count, local_width),
        ],
        axis=1,
    )
    b_query_grad = jnp.sum(joined_grad[:, :local_width].astype(jnp.float32), axis=0)
    b_value_grad = jnp.sum(joined_grad[:, 2 * local_width :].astype(jnp.float32), axis=0)
    projection_grad = outer_sum(tokens, joined_grad)
    token_part = back_product(joined_grad, joined).astype(jnp.bfloat16)
    summed_rows = first_grad + lax.psum(token_part, "mp").astype(jnp.float32)
    tokens_grad = lax.dynamic_slice_in_dim(summed_rows, offset, share, 0).astype(jnp.bfloat16)
    summed = (
        lax.psum_scatter(projection_grad[:, :local_width], "dp", scatter_dimension=0, tiled=True),
        lax.psum_scatter(
            projection_grad[:, local_width : 2 * local_width], "dp", scatter_dimension=0, tiled=True
        ),
        lax.psum_scatter(
            projection_grad[:, 2 * local_width :], "dp", scatter_dimension=0, tiled=True
        ),
        lax.psum_scatter(w_up_grad, "dp", scatter_dimension=0, tiled=True),
        lax.psum_scatter(w_out_grad, "dp", scatter_dimension=1, tiled=True),
        lax.psum_scatter(w_down_grad, "dp", scatter_dimension=1, tiled=True),
        lax.psum_scatter(b_query_grad, "dp", scatter_dimension=0, tiled=True),
        lax.psum_scatter(b_value_grad, "dp", scatter_dimension=0, tiled=True),
        lax.psum_scatter(b_up_grad, "dp", scatter_dimension=0, tiled=True),
        lax.psum_scatter(b_out_grad, "dp", scatter_dimension=0, tiled=True),
        lax.psum_scatter(b_down_grad, "dp", scatter_dimension=0, tiled=True),
    )
    norms = (
        lax.psum_scatter(mixed_gain_grad, ("dp", "mp"), scatter_dimension=0, tiled=True),
        lax.psum_scatter(mixed_shift_grad, ("dp", "mp"), scatter_dimension=0, tiled=True),
        lax.psum_scatter(final_gain_grad, ("dp", "mp"), scatter_dimension=0, tiled=True),
        lax.psum_scatter(final_shift_grad, ("dp", "mp"), scatter_dimension=0, tiled=True),
    )
    return (
        layer_out,
        tokens_grad,
        summed[0],
        summed[1],
        summed[2],
        summed[6],
        summed[7],
        summed[4],
        summed[9],
        norms[0],
        norms[1],
        summed[3],
        summed[8],
        summed[5],
        summed[10],
        norms[2],
        norms[3],
    )


def solution(mesh):
    placed = (
        P("dp", None),
        P("dp", None),
        P("dp", None),
        P("dp", None),
        P("dp", None),
        P(None, "mp"),
        P(None, "mp"),
        P(None, "mp"),
        P("mp"),
        P("mp"),
        P("mp", None),
        P(),
        P(),
        P(),
        P(None, "mp"),
        P("mp"),
        P("mp", None),
        P(),
        P(),
        P(),
    )
    return jax.shard_map(
        body,
        mesh=mesh,
        in_specs=placed,
        out_specs=(
            P(("dp", "mp"), None),
            P(("dp", "mp"), None),
            P("dp", "mp"),
            P("dp", "mp"),
            P("dp", "mp"),
            P(("mp", "dp")),
            P(("mp", "dp")),
            P("mp", "dp"),
            P("dp"),
            P(("dp", "mp")),
            P(("dp", "mp")),
            P("dp", "mp"),
            P(("mp", "dp")),
            P("mp", "dp"),
            P("dp"),
            P(("dp", "mp")),
            P(("dp", "mp")),
        ),
        check_vma=False,
    )
```

profile of v0, /device:TPU:0, one launch (start us, length us, event | category | flops | bytes accessed | tf_op | source)
XLA Modules:
  0.0 1006.0 jit_solution(596630303659771643)
XLA Ops:
  10.8 5.2 convolution_bitcast_fusion
  26.0 3.8 reshape.209
  33.4 30.0 %while.26 = (s32[]{:T(128)}, bf16[6,512,3,64]{1,3,2,0:T(8,128)(2,1)}, f32[6,3,512]{2,1,0:T(4,128)}, bf16[6,512,3,64]{1,3,2,0:T(8,128)(2,1)}, s32[6,512]{1,0:T(8,...) while((s32[]{:T(128)}, ...), condition=%wide.region_4.5_spmd, body=%wide.region_1.4_spmd.sunk | while | flops 211024384 | bytes 11528293 | solution.py:143
  71.9 96.4 %all-reduce.16.cloned.1.call-done = bf16[3072,768]{1,0:T(8,128)(2,1)} async-done(((bf16[3072,768]{1,0:T(8,128)(2,1)}), bf16[3072,768]{1,0:T(8,128)(2,1)}) %all-reduce.16.cloned.1.call-update) | async-done | bytes 4718608 | tf_op jit(solution)/shard_map/psum | solution.py:148
  168.3 5.5 fusion.70
  173.9 5.3 multiply_reduce_fusion.4
  181.8 25.0 %fusion.55 = (bf16[3072,768]{1,0:T(8,128)(2,1)S(1)}, f32[3072,768]{1,0:T(8,128)}) fusion(f32[768]{0:T(1024)S(1)} %copy-done.36, bf16[768,768]{1,0:T(8,128)(2,1)S(1)} %copy-done, f32[3072,768]{1,0:T(8,128)S(1)} %subtract_multiply_fusion.3, f32[768]{0:T(1024)S(1)} %copy-done.25, f32[768]{0:T(1024)S(1)} %copy-done.17), kind=kOutput, calls=%fused_computation.65 | convolution fusion | flops 3786670080 | bytes 24781824 | tf_op jit(solution)/shard_map/dot_general | solution.py:151
  209.0 5.5 convolution_convert_fusion.1
  214.8 94.1 %all-reduce.18.cloned.1.call-done = bf16[3072,768]{1,0:T(8,128)(2,1)} async-done(((bf16[3072,768]{1,0:T(8,128)(2,1)}), bf16[3072,768]{1,0:T(8,128)(2,1)}) %all-reduce.18.cloned.1.call-update) | async-done | bytes 4718608 | tf_op jit(solution)/shard_map/psum | solution.py:154
  308.9 7.2 fusion.78
  318.0 3.8 multiply_reduce_fusion.3
  321.8 9.2 multiply_reduce_fusion.6
  331.0 7.8 convert_reduce_fusion
  338.8 11.4 %convert_reduce_fusion.1 = (f32[768]{0:T(1024)}, bf16[3072,768]{1,0:T(8,128)(2,1)S(1)}) fusion(f32[3072,768]{1,0:T(8,128)} %get-tuple-element.319, f32[768]{0:T(1024)S(1)} %copy-done.36, bf16[768,768]{1,0:T(8,128)(2,1)S(1)} %copy-done.35, f32[3072,768]{1,0:T(8,128)S(1)} %get-tuple-element.302), kind=kOutput, calls=%fused_computation.73 | convolution fusion | flops 3656908032 | bytes 24778752 | tf_op jit(solution)/shard_map/dot_general | solution.py:57
  352.4 5.6 convolution_convert_fusion
  358.1 94.3 %all-reduce.20.cloned.1.call-done = bf16[3072,768]{1,0:T(8,128)(2,1)} async-done(((bf16[3072,768]{1,0:T(8,128)(2,1)}), bf16[3072,768]{1,0:T(8,128)(2,1)}) %all-reduce.20.cloned.1.call-update) | async-done | bytes 4718608 | tf_op jit(solution)/shard_map/psum | solution.py:170
  452.3 9.1 multiply_reduce_fusion.5
  461.4 9.6 convert_reduce_fusion.2
  477.7 5.4 convolution_convert_fusion.4
  487.6 61.8 %while.27 = (s32[]{:T(128)}, bf16[6,512,3,64]{1,3,2,0:T(8,128)(2,1)}, bf16[6,512,3,64]{1,3,2,0:T(8,128)(2,1)}, bf16[6,512,3,64]{1,3,2,0:T(8,128)(2,1)S(1)}, bf16...) while((s32[]{:T(128)}, ...), condition=%wide.region_18.19_spmd, body=%wide.region_16.18_spmd.sunk | while | flops 511146496 | bytes 26125436 | solution.py:180
  556.3 5.6 convolution_convert_fusion.2
  562.1 6.3 convolution_bitcast_fusion.1
  574.2 10.6 %fusion.82 = f32[768,768]{0,1:T(8,128)} fusion(bf16[3072,768]{1,0:T(8,128)(2,1)} %copy-done.39, f32[3072,768]{1,0:T(8,128)} %copy-done.8), kind=kOutput, calls=%fused_computation.155 | convolution fusion | flops 3626237952 | bytes 16515072 | tf_op jit(solution)/shard_map/dot_general | solution.py:51
  584.9 10.5 %fusion.74 = f32[768,768]{1,0:T(8,128)} fusion(bf16[3072,768]{1,0:T(8,128)(2,1)} %copy-done.38, f32[3072,768]{1,0:T(8,128)} %copy-done.1, f32[768]{0:T(1024)S(1)} %copy-done.26, f32[768]{0:T(1024)S(1)} %copy-done.18), kind=kOutput, calls=%fused_computation.129 | convolution fusion | flops 3630956544 | bytes 16521216 | tf_op jit(solution)/shard_map/dot_general | solution.py:51
  597.3 3.9 dynamic-slice_reduce_fusion
  604.7 40.4 %all-reduce.9 = (f32[768]{0:T(1024)}, f32[768]{0:T(1024)}, f32[768]{0:T(1024)}, f32[768]{0:T(1024)}) all-reduce(f32[768]{0:T(1024)} %get-tuple-element.255, f32[768]{0:T(1024)} %get-tuple-element.254, f32[768]{0:T(1024)S(1)} %get-tuple-element.253, f32[768]{0:T(1024)S(1)} %get-tuple-element.252), channel_id=9, replica_groups=mesh['dp'=8,'mp'=4] {'dp','mp'}, use_global_device_ids=true, to_apply=%region_31.32.clone | all-reduce | flops 3072 | bytes 24576
  650.8 37.6 %all-reduce.10 = (f32[192]{0:T(256)S(1)}, f32[192]{0:T(256)S(1)}, f32[768]{0:T(1024)S(1)}, f32[768]{0:T(1024)S(1)}, f32[768]{0:T(1024)S(1)}) all-reduce(f32[192]{0:T(256)S(1)} %reduce_sum.184, f32[192]{0:T(256)S(1)} %reduce_sum.186, f32[768]{0:T(1024)S(1)} %copy-done.28, ...), channel_id=5, replica_groups=mesh['dp'=8,'mp'=4] {'dp'}, use_global_device_ids=true, to_apply=%region_24.25.clone | all-reduce | flops 2688 | bytes 21504
  696.1 27.7 %reduce-scatter.23.cloned.1.call-done = f32[96,192]{1,0:T(8,128)} async-done(((f32[768,192]{1,0:T(8,128)}), f32[96,192]{1,0:T(8,128)}) %reduce-scatter.23.cloned.1.call-update) | async-done | bytes 73744
  723.9 65.3 %reduce-scatter.21.cloned.1.call-done = f32[96,192]{1,0:T(8,128)} async-done(((f32[768,192]{1,0:T(8,128)}), f32[96,192]{1,0:T(8,128)}) %reduce-scatter.21.cloned.1.call-update) | async-done | bytes 73744
  789.1 65.7 %reduce-scatter.19.cloned.1.call-done = f32[96,192]{1,0:T(8,128)} async-done(((f32[768,192]{1,0:T(8,128)}), f32[96,192]{1,0:T(8,128)}) %reduce-scatter.19.cloned.1.call-update) | async-done | bytes 73744
  854.9 72.1 %reduce-scatter.17.cloned.1.call-done = f32[768,96]{0,1:T(8,128)} async-done(((f32[768,768]{0,1:T(8,128)}), f32[768,96]{0,1:T(8,128)}) %reduce-scatter.17.cloned.1.call-update) | async-done | bytes 294928 | tf_op jit(solution)/shard_map/reduce_scatter | solution.py:208
  927.0 72.0 %reduce-scatter.15.cloned.1.call-done = f32[96,768]{1,0:T(8,128)} async-done(((f32[768,768]{1,0:T(8,128)}), f32[96,768]{1,0:T(8,128)}) %reduce-scatter.15.cloned.1.call-update) | async-done | bytes 294928 | tf_op jit(solution)/shard_map/reduce_scatter | solution.py:206
  (261 shorter events, 167.8 us)
Async XLA Ops:
  7.2 174.6 %copy-start = (bf16[768,768]{1,0:T(8,128)(2,1)S(1)}, bf16[768,768]{1,0:T(8,128)(2,1)}, u32[]{:S(2)}) copy-start(bf16[768,768]{1,0:T(8,128)(2,1)} %param.38) | copy-start | bytes 3538948
  7.2 161.1 %all-reduce.16.cloned.1.call-start = ((), (), s32[]{:S(2)}) async-start(), calls=%async_computation.6 | async-start | bytes 9437184 | tf_op jit(solution)/shard_map/psum | solution.py:148
  24.2 8.4 copy-start.29
  24.2 8.4 copy-start.31
  24.2 8.4 copy-start.32
  63.4 8.0 copy-start.12
  71.4 96.9 %copy-start.23 = (f32[768]{0:T(1024)S(1)}, f32[768]{0:T(1024)}, u32[]{:S(2)}) copy-start(f32[768]{0:T(1024)} %param.35) | copy-start | bytes 9220
  71.4 237.4 %all-reduce.18.cloned.1.call-start = ((), (), s32[]{:S(2)}) async-start(), calls=%async_computation.7 | async-start | bytes 9437184 | tf_op jit(solution)/shard_map/psum | solution.py:154
  168.3 10.9 %slice-start = ((s8[4718592]{0:T(1024)(128)(4,1)}), s8[524288]{0:T(1024)(128)(4,1)S(1)}, s32[]{:S(2)}) async-start(s8[4718592]{0:T(1024)(128)(4,1)} %bitcast.164), calls=%async_computation.16 | async-start | bytes 1048576
  181.8 25.0 %copy-start.1 = (f32[3072,768]{1,0:T(8,128)}, f32[3072,768]{1,0:T(8,128)S(1)}, u32[]{:S(2)}) copy-start(f32[3072,768]{1,0:T(8,128)S(1)} %subtract_multiply_fusion.3) | copy-start | bytes 28311556
  181.8 27.2 %copy-start.35 = (bf16[768,768]{1,0:T(8,128)(2,1)S(1)}, bf16[768,768]{1,0:T(8,128)(2,1)}, u32[]{:S(2)}) copy-start(bf16[768,768]{1,0:T(8,128)(2,1)} %param.40) | copy-start | bytes 3538948
  214.5 94.4 %copy-start.24 = (f32[768]{0:T(1024)S(1)}, f32[768]{0:T(1024)}, u32[]{:S(2)}) copy-start(f32[768]{0:T(1024)} %param.41) | copy-start | bytes 9220
  214.5 237.8 %all-reduce.20.cloned.1.call-start = ((), (), s32[]{:S(2)}) async-start(), calls=%async_computation.8 | async-start | bytes 9437184 | tf_op jit(solution)/shard_map/psum | solution.py:170
  308.9 9.1 copy-start.7
  338.8 11.4 %copy-start.8 = (f32[3072,768]{1,0:T(8,128)}, f32[3072,768]{1,0:T(8,128)S(1)}, u32[]{:S(2)}) copy-start(f32[3072,768]{1,0:T(8,128)S(1)} %get-tuple-element.302) | copy-start | bytes 28311556
  358.0 333.3 %reduce-scatter.25.cloned.1.call-start = ((), (), s32[]{:S(2)}) async-start(), calls=%async_computation.15 | async-start | bytes 884736
  461.4 9.7 copy-start.4
  461.4 13.3 %copy-start.10 = (bf16[24,8,6,512]{3,1,2,0:T(8,128)(2,1)S(1)}, bf16[24,8,6,512]{3,1,2,0:T(8,128)(2,1)}, u32[]{:S(2)}) copy-start(bf16[24,8,6,512]{3,1,2,0:T(8,128)(2,1)} %copy-done.9) | copy-start | bytes 3538948
  483.1 209.8 %all-reduce.22.cloned.1.call-start = ((), (), s32[]{:S(2)}) async-start(), calls=%async_computation.9 | async-start | bytes 9437184 | tf_op jit(solution)/shard_map/psum | solution.py:196
  561.9 162.0 %reduce-scatter.23.cloned.1.call-start = ((), (), s32[]{:S(2)}) async-start(), calls=%async_computation.14 | async-start | bytes 884736
  571.6 217.6 %reduce-scatter.21.cloned.1.call-start = ((), (), s32[]{:S(2)}) async-start(), calls=%async_computation.13 | async-start | bytes 884736
  572.9 282.0 %reduce-scatter.19.cloned.1.call-start = ((), (), s32[]{:S(2)}) async-start(), calls=%async_computation.12 | async-start | bytes 884736
  574.1 10.8 %copy-start.18 = (f32[768]{0:T(1024)S(1)}, f32[768]{0:T(1024)}, u32[]{:S(2)}) copy-start(f32[768]{0:T(1024)} %param.36) | copy-start | bytes 9220
  574.1 10.8 %copy-start.26 = (f32[768]{0:T(1024)S(1)}, f32[768]{0:T(1024)}, u32[]{:S(2)}) copy-start(f32[768]{0:T(1024)} %param.37) | copy-start | bytes 9220
  574.1 352.8 %reduce-scatter.17.cloned.1.call-start = ((), (), s32[]{:S(2)}) async-start(), calls=%async_computation.11 | async-start | bytes 2654208 | tf_op jit(solution)/shard_map/reduce_scatter | solution.py:208
  584.8 10.6 %copy-start.37 = (u32[32]{0:T(128)S(1)}, u32[32]{0:T(128)}, u32[]{:S(2)}) copy-start(u32[32]{0:T(128)} %constant.147) | copy-start | bytes 388
  584.8 12.5 %copy-start.22 = (f32[768]{0:T(1024)S(1)}, f32[768]{0:T(1024)}, u32[]{:S(2)}) copy-start(f32[768]{0:T(1024)} %param.42) | copy-start | bytes 9220
  584.8 12.5 %copy-start.30 = (f32[768]{0:T(1024)S(1)}, f32[768]{0:T(1024)}, u32[]{:S(2)}) copy-start(f32[768]{0:T(1024)} %param.43) | copy-start | bytes 9220
  584.8 414.1 %reduce-scatter.15.cloned.1.call-start = ((), (), s32[]{:S(2)}) async-start(), calls=%async_computation.10 | async-start | bytes 2654208 | tf_op jit(solution)/shard_map/reduce_scatter | solution.py:206
  597.3 53.1 %copy-start.13 = (bf16[6,512,3,64]{1,3,2,0:T(8,128)(2,1)S(1)}, bf16[6,512,3,64]{1,3,2,0:T(8,128)(2,1)}, u32[]{:S(2)}) copy-start(bf16[6,512,3,64]{1,3,2,0:T(8,128)(2,1)} %get-tuple-element.111) | copy-start | bytes 3538948
  601.3 49.5 %copy-start.27 = (f32[768]{0:T(1024)S(1)}, f32[768]{0:T(1024)}, u32[]{:S(2)}) copy-start(f32[768]{0:T(1024)} %get-tuple-element.301) | copy-start | bytes 9220
  601.3 49.5 %copy-start.28 = (f32[768]{0:T(1024)S(1)}, f32[768]{0:T(1024)}, u32[]{:S(2)}) copy-start(f32[768]{0:T(1024)} %get-tuple-element.303) | copy-start | bytes 9220
  (20 other events, 82.7 us)
Sparse Core Ops, SparseCore 0:
  71.5 96.7 all-reduce.15
  214.7 94.1 all-reduce.17
  358.1 94.1 all-reduce.19
  483.2 62.7 reduce-scatter.24
  562.0 95.0 all-reduce.21
  661.2 62.6 reduce-scatter.22
  727.7 61.3 reduce-scatter.20
  793.4 61.4 reduce-scatter.18
  858.9 67.9 reduce-scatter.16
  930.9 68.0 reduce-scatter.14
where the time goes:
time: 1020 us; the launch traced here: 1010 us
  waiting for transfers between devices  588 us (58%)
  matrix products  169 us (17%)
  other arithmetic  89.5 us (9%)
  blocking collectives  78 us (8%)
  local copies, waits for them, and re-layouts  63.2 us (6%)
  between operations  16.3 us (2%)
    unnamed x14, waiting for transfers between devices  159 us
    psum x1, waiting for transfers between devices, body(): lax.psum(attention_part, 'mp').astype(jnp.float32)  96.4 us
    psum x1, waiting for transfers between devices, body(): normed_grad = second_grad + lax.psum(normed_part, 'mp').astype(jnp.float32)  94.3 us
    psum x1, waiting for transfers between devices, body(): second = normed + lax.psum(down_part, 'mp').astype(jnp.float32) + b_down  94.1 us
    unnamed x2, blocking collectives  78 us
    reduce_scatter x1, waiting for transfers between devices, body(): lax.psum_scatter(w_down_grad, 'dp', scatter_dimension=1, tiled=True)  72.1 us
    reduce_scatter x1, waiting for transfers between devices, body(): lax.psum_scatter(w_up_grad, 'dp', scatter_dimension=0, tiled=True)  72 us
    unnamed x106, local copies, waits for them, and re-layouts  31.6 us
  transfers between devices with their start and end apart: 10, of which 8 were waited for; matrix products, arithmetic and copies ran while one was open for 13% of the time, Pallas kernels for 0%

commit v1 on v0

v1 whole, which is shorter than its diff:
```python
import functools

import jax
import jax.numpy as jnp
from jax import lax
from jax.experimental import pallas as pl
from jax.experimental.pallas import tpu as pltpu
from jax.sharding import PartitionSpec as P

HD = 64
BIN = 512
SLOTS = 12
WIDE = 256
CHUNK = 256

EPS = 1e-05
NEG = -1e30
ROOT_HALF = 0.7071067811865476
DENSITY = 0.3989422804014327

F32 = jnp.float32
BF16 = jnp.bfloat16


def mm(a, b):
    return lax.dot_general(a, b, (((1,), (0,)), ((), ())), preferred_element_type=F32)


def mm_nt(a, b):
    return lax.dot_general(a, b, (((1,), (1,)), ((), ())), preferred_element_type=F32)


def mm_tn(a, b):
    return lax.dot_general(a, b, (((0,), (0,)), ((), ())), preferred_element_type=F32)


def shape(dims, dtype):
    return jax.ShapeDtypeStruct(dims, dtype)


def call(body, name, grid, ins, outs, out_shape, args, prefetch=0, scratch=(), aliases=None, flops=0, size=0, trans=0):
    return pl.pallas_call(
        body,
        name=name,
        grid_spec=pltpu.PrefetchScalarGridSpec(
            num_scalar_prefetch=prefetch, grid=grid, in_specs=ins, out_specs=outs, scratch_shapes=list(scratch)
        ),
        out_shape=out_shape,
        input_output_aliases=aliases or {},
        compiler_params=pltpu.CompilerParams(dimension_semantics=("arbitrary",) * len(grid)),
        cost_estimate=pl.CostEstimate(flops=flops, bytes_accessed=size, transcendentals=trans),
    )(*args)


def labels_at(places, block, start_ref, finish_ref):
    found = jnp.zeros_like(places)
    for slot in range(SLOTS):
        inside = (places >= start_ref[block, slot]) & (places < finish_ref[block, slot])
        found = jnp.where(inside, slot + 1, found)
    return found


def attend_forward(meta, starts, finishes, x0, x1, xq, a_ref, bq, bv, *refs):
    q_out, k_out, v_out, e_out, m_out, i_out, a_out = refs[-7:]
    step = pl.program_id(0)
    parity = meta[2]

    @pl.when(step == 0)
    def _():
        lane = lax.broadcasted_iota(jnp.int32, (BIN, WIDE), 1)
        for half, x in enumerate((x0, x1)):
            rows = x[...]
            k_out[0, half] = mm_nt(rows, a_ref[192:448, :]).astype(BF16)
            values = mm_nt(rows, a_ref[384:640, :]) + bv[...]
            v_out[0, half] = jnp.where(lane < 192, values, 1.0).astype(BF16)
        a_out[0] = a_ref[...]

    place = step + parity
    block = place // 2
    queries = (mm_nt(xq[...], a_ref[0:256, :]) + bq[...]).astype(BF16) * jnp.asarray(HD**-0.5, BF16)
    low_lane = lax.broadcasted_iota(jnp.int32, (CHUNK, 128), 1) < HD
    q0, q1 = queries[:, :128], queries[:, 128:]
    zero = jnp.zeros_like(q0)
    masked = (jnp.where(low_lane, q0, zero), jnp.where(low_lane, zero, q0), jnp.where(low_lane, q1, zero))
    for head in range(3):
        q_out[0, head] = masked[head]
    rows_at = lax.broadcasted_iota(jnp.int32, (CHUNK, 1), 0) + CHUNK * lax.rem(place, 2)
    cols_at = lax.broadcasted_iota(jnp.int32, (1, BIN), 1)
    here = meta[0] + block
    allowed = labels_at(rows_at, here, starts, finishes) == labels_at(cols_at, here, starts, finishes)
    v0 = v_out[0, block, :, 0:128]
    low_wide = lax.broadcasted_iota(jnp.int32, (BIN, 128), 1) < HD
    one = jnp.ones_like(v0)
    padded = (jnp.where(low_wide, v0, one), jnp.where(low_wide, one, v0), v_out[0, block, :, 128:256])
    sums = []
    for head in range(3):
        tile = slice(0, 128) if head < 2 else slice(128, 256)
        scores = mm_nt(masked[head], k_out[0, block, :, tile])
        scores = jnp.where(allowed, scores, NEG)
        highest = jnp.max(scores, axis=1, keepdims=True)
        expo = jnp.exp(scores - highest).astype(BF16)
        e_out[0, head] = expo
        sums.append(mm(expo, padded[head]))
    whole0 = jnp.where(low_lane, sums[0], sums[1])
    total0 = pltpu.roll(jnp.where(low_lane, sums[1], sums[0]), HD, 1)
    inv0 = 1.0 / total0
    total1 = pltpu.roll(sums[2], HD, 1)
    inv1 = jnp.where(low_lane, 1.0 / total1, 0.0)
    m_out[0, :, 0:128] = (whole0 * inv0).astype(BF16)
    m_out[0, :, 128:256] = (sums[2] * inv1).astype(BF16)
    i_out[0, :, 0:128] = inv0
    i_out[0, :, 128:256] = inv1


def forward_attention(group, meta, starts, finishes, tokens, weight, bq, bv, before):
    keep = lambda *block: pl.BlockSpec(block, lambda i, *_: (0,) * len(block))
    rows = 3 * CHUNK
    out_shape = [
        shape((4, 3, rows, 128), BF16),
        shape((4, 2, BIN, WIDE), BF16),
        shape((4, 2, BIN, WIDE), BF16),
        shape((4, 3, rows, BIN), BF16),
        shape((4, rows, WIDE), BF16),
        shape((4, rows, WIDE), F32),
        shape((4, 768, 768), BF16),
    ]
    outs = [
        pl.BlockSpec((1, 3, CHUNK, 128), lambda i, *_: (group, 0, i, 0)),
        pl.BlockSpec((1, 2, BIN, WIDE), lambda i, *_: (group, 0, 0, 0)),
        pl.BlockSpec((1, 2, BIN, WIDE), lambda i, *_: (group, 0, 0, 0)),
        pl.BlockSpec((1, 3, CHUNK, BIN), lambda i, *_: (group, 0, i, 0)),
        pl.BlockSpec((1, CHUNK, WIDE), lambda i, *_: (group, i, 0)),
        pl.BlockSpec((1, CHUNK, WIDE), lambda i, *_: (group, i, 0)),
        pl.BlockSpec((1, 768, 768), lambda i, *_: (group, 0, 0)),
    ]
    ins = [
        pl.BlockSpec((BIN, 768), lambda i, meta, *_: (meta[0], 0)),
        pl.BlockSpec((BIN, 768), lambda i, meta, *_: (meta[0] + 1, 0)),
        pl.BlockSpec((CHUNK, 768), lambda i, meta, *_: (meta[1] + i, 0)),
        keep(768, 768),
        keep(1, WIDE),
        keep(1, WIDE),
    ]
    args = [meta, starts, finishes, tokens, tokens, tokens, weight, bq, bv]
    aliases = {}
    if before is not None:
        for position, array in enumerate(before):
            aliases[len(args)] = position
            args.append(array)
            ins.append(pl.BlockSpec(memory_space=pl.ANY))
    return call(
        attend_forward,
        "attend_forward",
        (3,),
        ins,
        outs,
        out_shape,
        args,
        prefetch=3,
        aliases=aliases,
        flops=3_500_000_000,
        size=9_000_000,
        trans=1_200_000,
    )


def project_norm(meta, m_ref, a_ref, x_ref, b_out, gain, shift, normal_out, inverse_out, low_out, lowt_out):
    total = x_ref[...].astype(F32) + b_out[...]
    for group in range(4):
        total += mm(m_ref[group, :, 0:192], a_ref[group])
    centered = total - jnp.mean(total, axis=-1, keepdims=True)
    inverse = lax.rsqrt(jnp.mean(centered * centered, axis=-1, keepdims=True) + EPS)
    normal = centered * inverse
    normal_out[...] = normal
    inverse_out[...] = jnp.broadcast_to(inverse, (CHUNK, 128))
    normed = normal * gain[...] + shift[...]
    low_out[...] = normed.astype(BF16)
    lowt_out[...] = normed.T.astype(BF16)


def project_and_norm(meta, mixed, weights, tokens, b_out, gain, shift):
    rows = 3 * CHUNK
    vector = pl.BlockSpec((1, 768), lambda i, *_: (0, 0))
    return call(
        project_norm,
        "project_norm",
        (3,),
        [
            pl.BlockSpec((4, CHUNK, WIDE), lambda i, *_: (0, i, 0)),
            pl.BlockSpec((4, 192, 768), lambda i, *_: (0, 3, 0)),
            pl.BlockSpec((CHUNK, 768), lambda i, meta, *_: (meta[1] + i, 0)),
            vector,
            vector,
            vector,
        ],
        [
            pl.BlockSpec((CHUNK, 768), lambda i, *_: (i, 0)),
            pl.BlockSpec((CHUNK, 128), lambda i, *_: (i, 0)),
            pl.BlockSpec((CHUNK, 768), lambda i, *_: (i, 0)),
            pl.BlockSpec((768, CHUNK), lambda i, *_: (0, i)),
        ],
        [shape((rows, 768), F32), shape((rows, 128), F32), shape((rows, 768), BF16), shape((768, rows), BF16)],
        [meta, mixed, weights, tokens, b_out, gain, shift],
        prefetch=1,
        flops=906_000_000,
        size=9_000_000,
    )


def feed_forward(x_ref, ua, ub, na, nb, ba, bb, *refs):
    hidden_out, slope_out, u_out, n_out, fed_out = refs[-5:]
    fed_in = refs[0]
    which, step = pl.program_id(0), pl.program_id(1)
    up = jnp.where(which == 0, ua[...], ub[...])
    down = jnp.where(which == 0, na[...], nb[...])
    bias = jnp.where(which == 0, ba[...], bb[...])
    u_out[0] = up
    n_out[0] = down

    @pl.when((which == 0) & (step == 0))
    def _():
        if len(refs) > 5:
            fed_out[...] = fed_in[...]
        else:
            fed_out[...] = jnp.zeros_like(fed_out)

    for part in range(3):
        rows = slice(part * CHUNK, (part + 1) * CHUNK)
        inner = mm(x_ref[rows, :], up) + bias
        half = 0.5 + 0.5 * lax.erf(inner * ROOT_HALF)
        hidden = (inner * half).astype(BF16)
        hidden_out[0, rows, :] = hidden
        slope_out[0, rows, :] = (half + inner * (jnp.exp(-0.5 * inner * inner) * DENSITY)).astype(BF16)
        fed_out[rows, :] += mm(hidden, down)


def forward_feed(side, low, ua, ub, na, nb, ba, bb, fed, before):
    rows = 3 * CHUNK
    first = lambda j, i: jnp.where(j == 0, i, 2)
    second = lambda j, i: jnp.where(j == 0, 0, i)
    ins = [
        pl.BlockSpec((rows, 768), lambda j, i: (0, 0)),
        pl.BlockSpec((768, CHUNK), lambda j, i: (0, first(j, i))),
        pl.BlockSpec((768, CHUNK), lambda j, i: (0, second(j, i))),
        pl.BlockSpec((CHUNK, 768), lambda j, i: (first(j, i), 0)),
        pl.BlockSpec((CHUNK, 768), lambda j, i: (second(j, i), 0)),
        pl.BlockSpec((1, CHUNK), lambda j, i: (0, first(j, i))),
        pl.BlockSpec((1, CHUNK), lambda j, i: (0, second(j, i))),
    ]
    args = [low, ua, ub, na, nb, ba, bb]
    aliases = {}
    if fed is not None:
        ins.append(pl.BlockSpec((rows, 768), lambda j, i: (0, 0)))
        args.append(fed)
        for position, array in enumerate(before):
            aliases[len(args)] = position
            args.append(array)
            ins.append(pl.BlockSpec(memory_space=pl.ANY))
    return call(
        feed_forward,
        "feed_forward",
        (2, 3),
        ins,
        [
            pl.BlockSpec((1, rows, CHUNK), lambda j, i: (2 * side + j, 0, i)),
            pl.BlockSpec((1, rows, CHUNK), lambda j, i: (2 * side + j, 0, i)),
            pl.BlockSpec((1, 768, CHUNK), lambda j, i: (2 * side + j, 0, i)),
            pl.BlockSpec((1, CHUNK, 768), lambda j, i: (2 * side + j, i, 0)),
            pl.BlockSpec((rows, 768), lambda j, i: (0, 0)),
        ],
        [
            shape((4, rows, 768), BF16),
            shape((4, rows, 768), BF16),
            shape((4, 768, 768), BF16),
            shape((4, 768, 768), BF16),
            shape((rows, 768), F32),
        ],
        args,
        aliases=aliases,
        flops=3_620_000_000,
        size=20_000_000,
        trans=2_400_000,
    )


def norm_around(meta, starts, finishes, fed, normal1, og, b_down, gain1, shift1, gain2, shift2, out, grad, low, lowt, sums):
    step = pl.program_id(0)
    second = normal1[...] * gain1[...] + shift1[...] + fed[...] + b_down[...]
    centered = second - jnp.mean(second, axis=-1, keepdims=True)
    inverse = lax.rsqrt(jnp.mean(centered * centered, axis=-1, keepdims=True) + EPS)
    normal = centered * inverse
    out[...] = (normal * gain2[...] + shift2[...]).astype(BF16)
    chunk = meta[1] + step
    rows_at = lax.broadcasted_iota(jnp.int32, (CHUNK, 1), 0) + CHUNK * lax.rem(chunk, 2)
    valid = labels_at(rows_at, chunk // 2, starts, finishes) > 0
    upstream = jnp.where(valid, og[...].astype(F32), 0.0)
    scaled = upstream * gain2[...]
    second_grad = inverse * (
        scaled
        - jnp.mean(scaled, axis=-1, keepdims=True)
        - normal * jnp.mean(scaled * normal, axis=-1, keepdims=True)
    )
    grad[...] = second_grad
    rounded = second_grad.astype(BF16)
    low[...] = rounded
    lowt[...] = second_grad.T.astype(BF16)

    @pl.when(step == 0)
    def _():
        sums[...] = jnp.zeros_like(sums)

    sums[0:1, :] += jnp.sum(upstream * normal, axis=0, keepdims=True)
    sums[1:2, :] += jnp.sum(upstream, axis=0, keepdims=True)
    sums[2:3, :] += jnp.sum(rounded.astype(F32), axis=0, keepdims=True)


def second_norm(meta, starts, finishes, fed, normal1, out_grad, b_down, gain1, shift1, gain2, shift2):
    rows = 3 * CHUNK
    vector = pl.BlockSpec((1, 768), lambda i, *_: (0, 0))
    tile = pl.BlockSpec((CHUNK, 768), lambda i, *_: (i, 0))
    return call(
        norm_around,
        "norm_around",
        (3,),
        [tile, tile, pl.BlockSpec((CHUNK, 768), lambda i, meta, *_: (meta[1] + i, 0))] + [vector] * 5,
        [tile, tile, tile, pl.BlockSpec((768, CHUNK), lambda i, *_: (0, i)), pl.BlockSpec((8, 768), lambda i, *_: (0, 0))],
        [
            shape((rows, 768), BF16),
            shape((rows, 768), F32),
            shape((rows, 768), BF16),
            shape((768, rows), BF16),
            shape((8, 768), F32),
        ],
        [meta, starts, finishes, fed, normal1, out_grad, b_down, gain1, shift1, gain2, shift2],
        prefetch=3,
        flops=20_000_000,
        size=12_000_000,
    )


def outer(left, right, out):
    out[0] = mm(left[...], right[0]).astype(BF16)


def outer_grads(odd, left, right):
    return call(
        outer,
        "outer_grads",
        (2, 2),
        [
            pl.BlockSpec((768, 768), lambda j, i: (0, 0)),
            pl.BlockSpec((1, 768, 384), lambda j, i: (2 * j + odd, 0, i)),
        ],
        pl.BlockSpec((1, 768, 384), lambda j, i: (j, 0, i)),
        shape((2, 768, 768), BF16),
        [left, right],
        flops=1_812_000_000,
        size=6_000_000,
    )


def feed_back(grad, slope, u_ref, n_ref, ig_out, ng_out, sums):
    group, step = pl.program_id(0), pl.program_id(1)

    @pl.when((group == 0) & (step == 0))
    def _():
        ng_out[...] = jnp.zeros_like(ng_out)

    total = jnp.zeros((1, CHUNK), F32)
    for part in range(3):
        rows = slice(part * CHUNK, (part + 1) * CHUNK)
        hidden_grad = mm_nt(grad[rows, :], n_ref[0])
        inner = (hidden_grad * slope[0, rows, :].astype(F32)).astype(BF16)
        ig_out[0, rows, :] = inner
        total += jnp.sum(inner.astype(F32), axis=0, keepdims=True)
        ng_out[rows, :] += mm_nt(inner, u_ref[0])
    sums[0] = jnp.broadcast_to(total, (8, CHUNK))


def backward_feed(grad, slope, ups, downs):
    rows = 3 * CHUNK
    return call(
        feed_back,
        "feed_back",
        (4, 3),
        [
            pl.BlockSpec((rows, 768), lambda j, i: (0, 0)),
            pl.BlockSpec((1, rows, CHUNK), lambda j, i: (j, 0, i)),
            pl.BlockSpec((1, 768, CHUNK), lambda j, i: (j, 0, i)),
            pl.BlockSpec((1, CHUNK, 768), lambda j, i: (j, i, 0)),
        ],
        [
            pl.BlockSpec((1, rows, CHUNK), lambda j, i: (j, 0, i)),
            pl.BlockSpec((rows, 768), lambda j, i: (0, 0)),
            pl.BlockSpec((1, 8, CHUNK), lambda j, i: (j, 0, i)),
        ],
        [shape((4, rows, 768), BF16), shape((rows, 768), F32), shape((4, 8, 768), F32)],
        [grad, slope, ups, downs],
        flops=7_240_000_000,
        size=25_000_000,
    )


def norm_back(ng, second, normal, inverse, gain, grad, low, lowt, sums):
    step = pl.program_id(0)
    total = ng[...] + second[...]
    normal1 = normal[...]
    scaled = total * gain[...]
    first = inverse[:, 0:1] * (
        scaled
        - jnp.mean(scaled, axis=-1, keepdims=True)
        - normal1 * jnp.mean(scaled * normal1, axis=-1, keepdims=True)
    )
    grad[...] = first
    rounded = first.astype(BF16)
    low[...] = rounded
    lowt[...] = first.T.astype(BF16)

    @pl.when(step == 0)
    def _():
        sums[...] = jnp.zeros_like(sums)

    sums[0:1, :] += jnp.sum(total * normal1, axis=0, keepdims=True)
    sums[1:2, :] += jnp.sum(total, axis=0, keepdims=True)
    sums[2:3, :] += jnp.sum(rounded.astype(F32), axis=0, keepdims=True)


def first_norm_back(ng, second, normal, inverse, gain):
    rows = 3 * CHUNK
    tile = pl.BlockSpec((CHUNK, 768), lambda i: (i, 0))
    return call(
        norm_back,
        "norm_back",
        (3,),
        [tile, tile, tile, pl.BlockSpec((CHUNK, 128), lambda i: (i, 0)), pl.BlockSpec((1, 768), lambda i: (0, 0))],
        [tile, tile, pl.BlockSpec((768, CHUNK), lambda i: (0, i)), pl.BlockSpec((8, 768), lambda i: (0, 0))],
        [shape((rows, 768), F32), shape((rows, 768), BF16), shape((768, rows), BF16), shape((8, 768), F32)],
        [ng, second, normal, inverse, gain],
        flops=20_000_000,
        size=12_000_000,
    )


def attend_backward(meta, ag, wo, q_ref, k_ref, v_ref, e_ref, m_ref, i_ref, dq_out, dk_own, dv_own, dk_far, dv_far, dk_acc, dv_acc):
    step = pl.program_id(1)
    parity = meta[2]
    block = (step + parity) // 2

    @pl.when(step == 0)
    def _():
        dk_acc[...] = jnp.zeros_like(dk_acc)
        dv_acc[...] = jnp.zeros_like(dv_acc)

    lane = lax.broadcasted_iota(jnp.int32, (CHUNK, 128), 1)
    low_lane = lane < HD
    mixed_grad = mm_nt(ag[...], wo[0]).astype(BF16).astype(F32)
    grad0 = mixed_grad[:, 0:128] * i_ref[0, :, 0:128]
    grad1 = jnp.concatenate([mixed_grad[:, 128:192], jnp.zeros((CHUNK, HD), F32)], axis=1) * i_ref[0, :, 128:256]
    prod0 = grad0 * m_ref[0, :, 0:128].astype(F32)
    prod1 = grad1 * m_ref[0, :, 128:256].astype(F32)
    centre = (
        jnp.sum(jnp.where(low_lane, prod0, 0.0), axis=1, keepdims=True),
        jnp.sum(jnp.where(low_lane, 0.0, prod0), axis=1, keepdims=True),
        jnp.sum(prod1, axis=1, keepdims=True),
    )
    v0 = v_ref[0, block, :, 0:128]
    low_wide = lax.broadcasted_iota(jnp.int32, (BIN, 128), 1) < HD
    one = jnp.ones_like(v0)
    padded = (jnp.where(low_wide, v0, one), jnp.where(low_wide, one, v0), v_ref[0, block, :, 128:256])
    dq = []
    for head in range(3):
        tile = slice(0, 128) if head < 2 else slice(128, 256)
        own = low_lane if head != 1 else ~low_lane
        base = HD if head != 1 else 0
        part = grad0 if head < 2 else grad1
        high = (-centre[head]).astype(BF16).astype(F32)
        rest = -centre[head] - high
        plain = jnp.where(own, part, 0.0)
        joined = jnp.where(lane == base, high, jnp.where(lane == base + 1, rest, plain)).astype(BF16)
        expo = e_ref[0, head]
        spread = mm_nt(joined, padded[head])
        score_grad = (expo.astype(F32) * spread).astype(BF16)
        dq.append(mm(score_grad, k_ref[0, block, :, tile]))
        dk_acc[block, :, tile] += mm_tn(score_grad, q_ref[0, head])
        dv_acc[block, :, tile] += mm_tn(expo, plain.astype(BF16))
    scale = HD**-0.5
    dq_out[0, :, 0:128] = (jnp.where(low_lane, dq[0], dq[1]) * scale).astype(BF16)
    dq_out[0, :, 128:256] = (dq[2] * scale).astype(BF16)

    @pl.when(step == 2)
    def _():
        for acc, own, far in ((dk_acc, dk_own, dk_far), (dv_acc, dv_own, dv_far)):
            for part in range(3):
                at = part + parity
                own[0, part * CHUNK : (part + 1) * CHUNK, :] = acc[
                    at // 2, pl.ds(pl.multiple_of(CHUNK * lax.rem(at, 2), CHUNK), CHUNK), :
                ].astype(BF16)
            at = 3 * (1 - parity)
            far[0] = acc[at // 2, pl.ds(pl.multiple_of(CHUNK * lax.rem(at, 2), CHUNK), CHUNK), :].astype(BF16)


def backward_attention(meta, attended_grad, weights, queries, keys, values, expo, mixed, inverses):
    rows = 3 * CHUNK
    return call(
        attend_backward,
        "attend_backward",
        (4, 3),
        [
            pl.BlockSpec((CHUNK, 768), lambda r, i, *_: (i, 0)),
            pl.BlockSpec((1, 192, 768), lambda r, i, *_: (r, 3, 0)),
            pl.BlockSpec((1, 3, CHUNK, 128), lambda r, i, *_: (r, 0, i, 0)),
            pl.BlockSpec((1, 2, BIN, WIDE), lambda r, i, *_: (r, 0, 0, 0)),
            pl.BlockSpec((1, 2, BIN, WIDE), lambda r, i, *_: (r, 0, 0, 0)),
            pl.BlockSpec((1, 3, CHUNK, BIN), lambda r, i, *_: (r, 0, i, 0)),
            pl.BlockSpec((1, CHUNK, WIDE), lambda r, i, *_: (r, i, 0)),
            pl.BlockSpec((1, CHUNK, WIDE), lambda r, i, *_: (r, i, 0)),
        ],
        [
            pl.BlockSpec((1, CHUNK, WIDE), lambda r, i, *_: (r, i, 0)),
            pl.BlockSpec((1, rows, WIDE), lambda r, i, *_: (r, 0, 0)),
            pl.BlockSpec((1, rows, WIDE), lambda r, i, *_: (r, 0, 0)),
            pl.BlockSpec((1, CHUNK, WIDE), lambda r, i, *_: (r, 0, 0)),
            pl.BlockSpec((1, CHUNK, WIDE), lambda r, i, *_: (r, 0, 0)),
        ],
        [
            shape((4, rows, WIDE), BF16),
            shape((4, rows, WIDE), BF16),
            shape((4, rows, WIDE), BF16),
            shape((4, CHUNK, WIDE), BF16),
            shape((4, CHUNK, WIDE), BF16),
        ],
        [meta, attended_grad, weights, queries, keys, values, expo, mixed, inverses],
        prefetch=1,
        scratch=[pltpu.VMEM((2, BIN, WIDE), F32), pltpu.VMEM((2, BIN, WIDE), F32)],
        flops=12_000_000_000,
        size=25_000_000,
    )


def project_back(meta, xt, agt, dq, dk, dv, far_k, far_v, mixed, a_ref, base, grads, tg_out, sums, joined):
    step = pl.program_id(0)
    joined[:, 0:192] = dq[0, :, 0:192]
    joined[:, 192:384] = dk[0, :, 0:192]
    joined[:, 384:576] = dv[0, :, 0:192]
    at = pl.ds(pl.multiple_of(2 * CHUNK * (1 - meta[2]), CHUNK), CHUNK)
    joined[at, 192:384] = (joined[at, 192:384].astype(F32) + far_k[0, :, 0:192].astype(F32)).astype(BF16)
    joined[at, 384:576] = (joined[at, 384:576].astype(F32) + far_v[0, :, 0:192].astype(F32)).astype(BF16)
    whole = joined[...]
    grads[0, :, 0:576] = mm(xt[...], whole).astype(BF16)
    grads[0, :, 576:768] = mm(agt[...], mixed[0, :, 0:192]).astype(BF16)
    sums[0, 0:1, :] = jnp.sum(whole.astype(F32), axis=0, keepdims=True)

    @pl.when(step == 0)
    def _():
        tg_out[...] = base[...]

    tg_out[...] += mm(whole, a_ref[0])


def backward_project(odd, meta, xt, agt, dq, dk, dv, far_k, far_v, mixed, weights, base):
    rows = 3 * CHUNK
    full = pl.BlockSpec((768, 768), lambda j, *_: (0, 0))
    per = pl.BlockSpec((1, rows, WIDE), lambda j, *_: (2 * j + odd, 0, 0))
    far = pl.BlockSpec((1, CHUNK, WIDE), lambda j, *_: (2 * j + 1 - odd, 0, 0))
    return call(
        project_back,
        "project_back",
        (2,),
        [
            full,
            full,
            per,
            per,
            per,
            far,
            far,
            per,
            pl.BlockSpec((1, 576, 768), lambda j, *_: (2 * j + odd, 0, 0)),
            full,
        ],
        [pl.BlockSpec((1, 768, 768), lambda j, *_: (j, 0, 0)), full, pl.BlockSpec((1, 8, 576), lambda j, *_: (j, 0, 0))],
        [shape((2, 768, 768), BF16), shape((rows, 768), F32), shape((2, 8, 576), F32)],
        [meta, xt, agt, dq, dk, dv, far_k, far_v, mixed, weights, base],
        prefetch=1,
        scratch=[pltpu.VMEM((rows, 576), BF16)],
        flops=3_200_000_000,
        size=20_000_000,
    )


def swap(array, bit, total):
    return lax.ppermute(array, ("dp", "mp"), [(i, i ^ bit) for i in range(total)])


def pick(array, index, axis):
    return lax.dynamic_index_in_dim(array, index, axis, keepdims=False)


def gather_group(own, total, parity):
    near = swap(own, 1, total)
    rows = own.shape[0] // 2
    part = lax.dynamic_slice_in_dim(own, parity * rows, rows, 0)
    over = swap(part, 2, total)
    other = swap(over, 4, total)
    far = jnp.where(
        parity == 0, jnp.concatenate([over, other], axis=0), jnp.concatenate([other, over], axis=0)
    )
    return own, near, far, swap(far, 1, total)


def halve(array, axis, bit, device_bit, total):
    sent = swap(pick(array, 1 - bit, axis), device_bit, total)
    return (pick(array, bit, axis).astype(F32) + sent.astype(F32)).astype(array.dtype)


def scatter_sum(kept, sent, place, total, n_dp):
    bits = [(place >> k) & 1 for k in range(n_dp.bit_length() - 1)]
    received = swap(sent, 1, total)
    both = (kept.astype(F32) + received.astype(F32)).astype(BF16)
    block = 768 // n_dp
    here = both[0, :, :384].astype(F32) + swap(both[1, :, :384], 2, total).astype(F32)
    here = here.astype(BF16).reshape(n_dp // 2, 2, block, 384)
    here = halve(here, 1, bits[0], 4, total)
    there = both[:, :, 384:].reshape(2, n_dp // 2, 2, block, 384)
    there = halve(there, 2, bits[0], 4, total)
    there = (there[0].astype(F32) + swap(there[1], 2, total).astype(F32)).astype(BF16)
    value = jnp.concatenate([here, there], axis=-1)
    left = n_dp // 2
    for k in range(1, len(bits)):
        value = value.reshape(left // 2, 2, block, 768)
        value = halve(value, 1, bits[k], 4 << k, total)
        left //= 2
    return value.reshape(block, 768)


def scatter_vectors(vectors, place, total, n_dp):
    value = vectors[0::2] + swap(vectors[1::2], 1, total)
    value = value[0] + swap(value[1], 2, total)
    left = n_dp
    for k in range(n_dp.bit_length() - 1):
        value = value.reshape(left // 2, 2, -1)
        value = halve(value, 1, (place >> k) & 1, 4 << k, total)
        left //= 2
    return value.reshape(-1)


def body(
    n_dp,
    tokens,
    out_grad,
    pair_start,
    caption_len,
    region_len,
    w_query,
    w_key,
    w_value,
    b_query,
    b_value,
    w_out,
    b_out,
    mixed_gain,
    mixed_shift,
    w_up,
    b_up,
    w_down,
    b_down,
    final_gain,
    final_shift,
):
    total = 4 * n_dp
    place, member = lax.axis_index("dp"), lax.axis_index("mp")
    parity = place & 1
    core = member & 1
    meta = jnp.stack([3 * (member // 2) + core, 3 * member, core]).astype(jnp.int32)
    finish = pair_start + caption_len + region_len
    row = lambda vector: vector.reshape(1, -1)

    attention_own = jnp.concatenate([w_query.T, w_key.T, w_value.T, w_out], axis=0)
    biases_own = jnp.concatenate([b_query, b_value, b_up])
    attention = gather_group(attention_own, total, parity)
    ups = gather_group(w_up, total, parity)
    downs = gather_group(w_down, total, parity)
    bias_near = swap(biases_own, 1, total)
    bias_far = swap(jnp.stack([biases_own, bias_near]), 2, total)
    biases = (biases_own, bias_near, bias_far[0], bias_far[1])
    wide = lambda vector: jnp.pad(vector, (0, WIDE - vector.shape[0])).reshape(1, WIDE)

    state = None
    for group in range(4):
        bias = biases[group]
        state = forward_attention(
            group, meta, pair_start, finish, tokens, attention[group], wide(bias[:192]), wide(bias[192:384]), state
        )
    queries, keys, values, expo, mixed, inverses, weights = state
    normal1, inverse1, low1, low1_t = project_and_norm(
        meta, mixed, weights, tokens, row(b_out), row(mixed_gain), row(mixed_shift)
    )
    fed, before = None, None
    for side in range(2):
        a, b = 2 * side, 2 * side + 1
        *before, fed = forward_feed(
            side, low1, ups[a], ups[b], downs[a], downs[b], row(biases[a][384:]), row(biases[b][384:]), fed, before
        )
    hidden, slope, up_all, down_all = before
    layer_out, second_grad, fed_grad, fed_grad_t, sums2 = second_norm(
        meta,
        pair_start,
        finish,
        fed,
        normal1,
        out_grad,
        row(b_down),
        row(mixed_gain),
        row(mixed_shift),
        row(final_gain),
        row(final_shift),
    )
    down_sent = outer_grads(1, fed_grad_t, hidden)
    down_kept = outer_grads(0, fed_grad_t, hidden)
    down_sum = scatter_sum(down_kept, down_sent, place, total, n_dp)
    inner_grad, normed_part, up_sums = backward_feed(fed_grad, slope, up_all, down_all)
    up_sent = outer_grads(1, low1_t, inner_grad)
    up_kept = outer_grads(0, low1_t, inner_grad)
    up_sum = scatter_sum(up_kept, up_sent, place, total, n_dp)
    first_grad, attended_grad, attended_grad_t, sums1 = first_norm_back(
        normed_part, second_grad, normal1, inverse1, row(mixed_gain)
    )
    dq, dk, dv, far_k, far_v = backward_attention(
        meta, attended_grad, weights, queries, keys, values, expo, mixed, inverses
    )
    got_k, got_v = swap(far_k, 1, total), swap(far_v, 1, total)
    own_tokens = lax.dynamic_slice_in_dim(tokens, member * 768, 768, 0)
    tokens_t = own_tokens.T
    heads_sent, partial, head_sums_sent = backward_project(
        1, meta, tokens_t, attended_grad_t, dq, dk, dv, got_k, got_v, mixed, weights, first_grad
    )
    heads_kept, whole, head_sums_kept = backward_project(
        0, meta, tokens_t, attended_grad_t, dq, dk, dv, got_k, got_v, mixed, weights, partial
    )
    tokens_grad = whole.astype(BF16)
    heads_sum = scatter_sum(heads_kept, heads_sent, place, total, n_dp)

    head_sums = jnp.stack([head_sums_kept[0, 0], head_sums_sent[0, 0], head_sums_kept[1, 0], head_sums_sent[1, 0]])
    small = 192 // n_dp
    block = 768 // n_dp
    spread = lambda vector: jnp.broadcast_to(vector.reshape(1, n_dp, block), (4, n_dp, block))
    by_member = lambda vector: jnp.stack([pick(vector.reshape(n_dp, 4, small), member ^ r, 1) for r in range(4)])
    vectors = jnp.concatenate(
        [
            head_sums[:, 0:192].reshape(4, n_dp, small),
            head_sums[:, 384:576].reshape(4, n_dp, small),
            up_sums[:, 0].reshape(4, n_dp, block),
            spread(sums1[2]),
            spread(sums2[2]),
            by_member(sums1[0]),
            by_member(sums1[1]),
            by_member(sums2[0]),
            by_member(sums2[1]),
        ],
        axis=2,
    )
    vector = scatter_vectors(vectors, place, total, n_dp)
    cuts, at = [], 0
    for length in (small, small, block, block, block, small, small, small, small):
        cuts.append(vector[at : at + length])
        at += length
    bq_grad, bv_grad, bup_grad, bout_grad, bdown_grad, mg_grad, ms_grad, fg_grad, fs_grad = cuts
    heads_sum = heads_sum.astype(F32)
    return (
        layer_out,
        tokens_grad,
        heads_sum[:, 0:192],
        heads_sum[:, 192:384],
        heads_sum[:, 384:576],
        bq_grad,
        bv_grad,
        heads_sum[:, 576:768].T,
        bout_grad,
        mg_grad,
        ms_grad,
        up_sum.astype(F32),
        bup_grad,
        down_sum.astype(F32).T,
        bdown_grad,
        fg_grad,
        fs_grad,
    )


def solution(mesh):
    n_dp = mesh.shape["dp"]
    placed = (
        P("dp", None),
        P("dp", None),
        P("dp", None),
        P("dp", None),
        P("dp", None),
        P(None, "mp"),
        P(None, "mp"),
        P(None, "mp"),
        P("mp"),
        P("mp"),
        P("mp", None),
        P(),
        P(),
        P(),
        P(None, "mp"),
        P("mp"),
        P("mp", None),
        P(),
        P(),
        P(),
    )
    return jax.shard_map(
        functools.partial(body, n_dp),
        mesh=mesh,
        in_specs=placed,
        out_specs=(
            P(("dp", "mp"), None),
            P(("dp", "mp"), None),
            P("dp", "mp"),
            P("dp", "mp"),
            P("dp", "mp"),
            P(("mp", "dp")),
            P(("mp", "dp")),
            P("mp", "dp"),
            P("dp"),
            P(("dp", "mp")),
            P(("dp", "mp")),
            P("dp", "mp"),
            P(("mp", "dp")),
            P("mp", "dp"),
            P("dp"),
            P(("dp", "mp")),
            P(("dp", "mp")),
        ),
        check_vma=False,
    )
```

time: 1020 us -> 357 us (0.35); the launches traced: 1010 us -> 355 us
  waiting for transfers between devices: 588 us -> 82.6 us
  Pallas kernels: 0 us -> 182 us
  matrix products: 169 us -> 0 us
  blocking collectives: 78 us -> 0 us
  other arithmetic: 89.5 us -> 21.6 us
  starting transfers between devices: 1.63 us -> 33.4 us
  local copies, waits for them, and re-layouts: 63.2 us -> 33.5 us
  between operations: 16.3 us -> 1.44 us
    psum x4 -> x0, waiting for transfers between devices: 285 us -> none  [the longest x1 96.4 us: body(): lax.psum(attention_part, 'mp').astype(jnp.float32)]
    pallas_call x0 -> x17, Pallas kernels: none -> 182 us  [call(): pl.pallas_call(body, name=name, grid_spec=pltpu.PrefetchScalarGridSpec(nu...]
    dot_general x53 -> x0, matrix products: 166 us -> none  [the longest x4 27.9 us: back_product(): lax.dot_general(gradient, weight, (((1,), (1,)), ((), ())), preferred_ele...]
    unnamed x14 -> x0, waiting for transfers between devices: 159 us -> none
    reduce_scatter x2 -> x0, waiting for transfers between devices: 144 us -> none  [the longest x1 72.1 us: body(): lax.psum_scatter(w_down_grad, 'dp', scatter_dimension=1, tiled=True)]
    ppermute x0 -> x42, waiting for transfers between devices: none -> 82.6 us  [swap(): lax.ppermute(array, ('dp', 'mp'), [(i, i ^ bit) for i in range(total)])]
    unnamed x2 -> x0, blocking collectives: 78 us -> none
    reduce_sum x18 -> x0, other arithmetic: 69.5 us -> none  [the longest x2 18.2 us: norm_back(): jnp.mean(scaled, axis=-1, keepdims=True)]
  transfers between devices with their start and end apart: 10 -> 42, of which waited for: 8 -> 17; matrix products, arithmetic and copies ran while one was open for 13% -> 13% of each run, Pallas kernels for 0% -> 24%
where the time goes in v1:
time: 357 us; the launch traced here: 355 us
  Pallas kernels  182 us (51%)
  waiting for transfers between devices  82.6 us (23%)
  local copies, waits for them, and re-layouts  33.5 us (9%)
  starting transfers between devices  33.4 us (9%)
  other arithmetic  21.6 us (6%)
    pallas_call x17, Pallas kernels, call(): pl.pallas_call(body, name=name, grid_spec=pltpu.PrefetchScalarGridSpec(nu...  182 us
    ppermute x42, waiting for transfers between devices, swap(): lax.ppermute(array, ('dp', 'mp'), [(i, i ^ bit) for i in range(total)])  82.6 us
    ppermute x42, starting transfers between devices, swap(): lax.ppermute(array, ('dp', 'mp'), [(i, i ^ bit) for i in range(total)])  33.4 us
    reshape x8, local copies, waits for them, and re-layouts, body(): row = lambda vector: vector.reshape(1, -1)  8.13 us
  transfers between devices with their start and end apart: 42, of which 17 were waited for; matrix products, arithmetic and copies ran while one was open for 13% of the time, Pallas kernels for 24%

profile of v1, /device:TPU:0, one launch (start us, length us, event | category | flops | bytes accessed | tf_op | source)
XLA Modules:
  0.0 354.6 jit_solution(2288265625905847941)
XLA Ops:
  3.5 3.0 collective-permute-start
  15.0 10.8 %attend_forward.4 = (bf16[4,3,768,128]{3,2,1,0:T(8,128)(2,1)}, bf16[4,2,512,256]{3,2,1,0:T(8,128)(2,1)}, bf16[4,2,512,256]{3,2,1,0:T(8,128)(2,1)}, bf16[4,3,768,...) custom-call(s32[3]{0:T(128)} %pad_add_fusion.meta, ...), custom_call_target="tpu_custom_call" | custom-call | flops 3500000000 | bytes 9000000 | tf_op jit(solution)/shard_map/attend_forward/pallas_call | solution.py:42
  47.4 3.0 maximum_select_fusion.a_ref
  53.3 8.2 %collective-permute-done.10 = bf16[384,768]{1,0:T(8,128)(2,1)S(1)} collective-permute-done((bf16[384,768]{1,0:T(8,128)(2,1)S(1)}, bf16[384,768]{1,0:T(8,128)(2,1)S(1)}, u32[]{:S(2)}, u32[]{:S(2)}) %collective-permute-start.10) | collective-permute-done | bytes 589856 | tf_op jit(solution)/shard_map/ppermute | solution.py:592
  62.1 10.6 %collective-permute-done.7 = bf16[384,768]{1,0:T(8,128)(2,1)S(1)} collective-permute-done((bf16[384,768]{1,0:T(8,128)(2,1)S(1)}, bf16[384,768]{1,0:T(8,128)(2,1)S(1)}, u32[]{:S(2)}, u32[]{:S(2)}) %collective-permute-start.7) | collective-permute-done | bytes 589856 | tf_op jit(solution)/shard_map/ppermute | solution.py:592
  74.9 10.8 %attend_forward.5 = (bf16[4,3,768,128]{3,2,1,0:T(8,128)(2,1)}, bf16[4,2,512,256]{3,2,1,0:T(8,128)(2,1)}, bf16[4,2,512,256]{3,2,1,0:T(8,128)(2,1)}, bf16[4,3,768,...) custom-call(s32[3]{0:T(128)} %pad_add_fusion.meta, ...), custom_call_target="tpu_custom_call", output_to_operand_aliasing={{0}: (9, {}), {1}: (10, {}), {2}: (11, {}), {3}: (12, {}), ... | custom-call | flops 3500000000 | bytes 9000000 | tf_op jit(solution)/shard_map/attend_forward/pallas_call | solution.py:42
  85.8 10.8 %attend_forward.6 = (bf16[4,3,768,128]{3,2,1,0:T(8,128)(2,1)}, bf16[4,2,512,256]{3,2,1,0:T(8,128)(2,1)}, bf16[4,2,512,256]{3,2,1,0:T(8,128)(2,1)}, bf16[4,3,768,...) custom-call(s32[3]{0:T(128)} %pad_add_fusion.meta, ...), custom_call_target="tpu_custom_call", output_to_operand_aliasing={{0}: (9, {}), {1}: (10, {}), {2}: (11, {}), {3}: (12, {}), ... | custom-call | flops 3500000000 | bytes 9000000 | tf_op jit(solution)/shard_map/attend_forward/pallas_call | solution.py:42
  96.7 10.8 %attend_forward.7 = (bf16[4,3,768,128]{3,2,1,0:T(8,128)(2,1)}, bf16[4,2,512,256]{3,2,1,0:T(8,128)(2,1)}, bf16[4,2,512,256]{3,2,1,0:T(8,128)(2,1)}, bf16[4,3,768,...) custom-call(s32[3]{0:T(128)} %pad_add_fusion.meta, ...), custom_call_target="tpu_custom_call", output_to_operand_aliasing={{0}: (9, {}), {1}: (10, {}), {2}: (11, {}), {3}: (12, {}), ... | custom-call | flops 3500000000 | bytes 9000000 | tf_op jit(solution)/shard_map/attend_forward/pallas_call | solution.py:42
  107.5 6.8 %project_norm.1 = (f32[768,768]{1,0:T(8,128)}, f32[768,128]{1,0:T(8,128)}, bf16[768,768]{1,0:T(8,128)(2,1)}, bf16[768,768]{1,0:T(8,128)(2,1)}) custom-call(s32[3]{0:T(128)} %pad_add_fusion.meta, bf16[4,768,256]{2,1,0:T(8,128)(2,1)} %get-tuple-element.103.m_ref.mixed, bf16[4,768,768]{2,1,0:T(8,128)(2,1)} %get-tuple-element.104.a_ref.wo, ...), custom_call_target="tpu_custom_call" | custom-call | flops 906000000 | bytes 9000000 | tf_op jit(solution)/shard_map/project_norm/pallas_call | solution.py:42
  114.3 11.7 %feed_forward.2 = (bf16[4,768,768]{2,1,0:T(8,128)(2,1)}, bf16[4,768,768]{2,1,0:T(8,128)(2,1)}, bf16[4,768,768]{2,1,0:T(8,128)(2,1)}, bf16[4,768,768]{2,1,0:T(8,128)(2,1)}, f32[768,768]{1,0:T(8,128)}) custom-call(bf16[768,768]{1,0:T(8,128)(2,1)} %get-tuple-element.105.x_ref, bf16[768,768]{1,0:T(8,128)(2,1)} %ua.1, ...), custom_call_target="tpu_custom_call" | custom-call | flops 3620000000 | bytes 20000000 | tf_op jit(solution)/shard_map/feed_forward/pallas_call | solution.py:42
  127.1 12.3 %feed_forward.3 = (bf16[4,768,768]{2,1,0:T(8,128)(2,1)}, bf16[4,768,768]{2,1,0:T(8,128)(2,1)}, bf16[4,768,768]{2,1,0:T(8,128)(2,1)}, bf16[4,768,768]{2,1,0:T(8,128)(2,1)}, f32[768,768]{1,0:T(8,128)}) custom-call(bf16[768,768]{1,0:T(8,128)(2,1)} %get-tuple-element.105.x_ref, ...), custom_call_target="tpu_custom_call", output_to_operand_aliasing={{0}: (8, {}), {1}: (9, {}), {2}: (10, {}), {3}: (11, {})} | custom-call | flops 3620000000 | bytes 20000000 | tf_op jit(solution)/shard_map/feed_forward/pallas_call | solution.py:42
  139.3 7.9 %norm_around.1 = (bf16[768,768]{1,0:T(8,128)(2,1)}, f32[768,768]{1,0:T(8,128)}, bf16[768,768]{1,0:T(8,128)(2,1)}, bf16[768,768]{1,0:T(8,128)(2,1)}, f32[8,768]{1,0:T(8,128)}) custom-call(s32[3]{0:T(128)} %pad_add_fusion.meta, s32[6,12]{1,0:T(8,128)} %starts.9, s32[6,12]{1,0:T(8,128)} %add_add_fusion.finishes, f32[768,768]{1,0:T(8,128)} %get-tuple-element.111.fed, ...), custom_call_target="tpu_custom_call" | custom-call | flops 20000000 | bytes 12000000 | tf_op jit(solution)/shard_map/norm_around/pallas_call | solution.py:42
  148.3 17.4 %feed_back.1 = (bf16[4,768,768]{2,1,0:T(8,128)(2,1)}, f32[768,768]{1,0:T(8,128)}, f32[4,8,768]{2,1,0:T(8,128)}) custom-call(bf16[768,768]{1,0:T(8,128)(2,1)} %get-tuple-element.114.grad, bf16[4,768,768]{2,1,0:T(8,128)(2,1)} %get-tuple-element.115.slope, bf16[4,768,768]{2,1,0:T(8,128)(2,1)} %get-tuple-element.116.u_ref, ...), custom_call_target="tpu_custom_call" | custom-call | flops 7240000000 | bytes 25000000 | tf_op jit(solution)/shard_map/feed_back/pallas_call | solution.py:42
  165.6 7.0 %norm_back.1 = (f32[768,768]{1,0:T(8,128)}, bf16[768,768]{1,0:T(8,128)(2,1)}, bf16[768,768]{1,0:T(8,128)(2,1)}, f32[8,768]{1,0:T(8,128)}) custom-call(f32[768,768]{1,0:T(8,128)} %get-tuple-element.118.ng, f32[768,768]{1,0:T(8,128)} %get-tuple-element.119.second, f32[768,768]{1,0:T(8,128)} %get-tuple-element.112.normal1.normal, ...), custom_call_target="tpu_custom_call" | custom-call | flops 20000000 | bytes 12000000 | tf_op jit(solution)/shard_map/norm_back/pallas_call | solution.py:42
  173.7 26.2 %attend_backward.1 = (bf16[4,768,256]{2,1,0:T(8,128)(2,1)}, bf16[4,768,256]{2,1,0:T(8,128)(2,1)}, bf16[4,768,256]{2,1,0:T(8,128)(2,1)}, bf16[4,256,256]{2,1,0:T(8,128)(2,1)}, bf16[4,256,256]{2,1,0:T(8,128)(2,1)}) custom-call(s32[3]{0:T(128)} %pad_add_fusion.meta, bf16[768,768]{1,0:T(8,128)(2,1)} %get-tuple-element.122.ag, ...), custom_call_target="tpu_custom_call" | custom-call | flops 12000000000 | bytes 25000000 | tf_op jit(solution)/shard_map/attend_backward/pallas_call | solution.py:42
  203.7 12.6 %project_back.2 = (bf16[2,768,768]{2,1,0:T(8,128)(2,1)}, f32[768,768]{1,0:T(8,128)}, f32[2,8,576]{2,1,0:T(8,128)}) custom-call(s32[3]{0:T(128)} %pad_add_fusion.meta, bf16[768,768]{1,0:T(8,128)(2,1)} %bitcast.206, bf16[768,768]{1,0:T(8,128)(2,1)} %get-tuple-element.121.agt, bf16[4,768,256]{2,1,0:T(8,128)(2,1)} %get-tuple-element.128.dq, ...), custom_call_target="tpu_custom_call" | custom-call | flops 3200000000 | bytes 20000000 | tf_op jit(solution)/shard_map/project_back/pallas_call | solution.py:42
  216.3 12.8 %project_back.3 = (bf16[2,768,768]{2,1,0:T(8,128)(2,1)}, f32[768,768]{1,0:T(8,128)}, f32[2,8,576]{2,1,0:T(8,128)}) custom-call(s32[3]{0:T(128)} %pad_add_fusion.meta, bf16[768,768]{1,0:T(8,128)(2,1)} %bitcast.207, bf16[768,768]{1,0:T(8,128)(2,1)} %get-tuple-element.121.agt, bf16[4,768,256]{2,1,0:T(8,128)(2,1)} %get-tuple-element.128.dq, ...), custom_call_target="tpu_custom_call" | custom-call | flops 3200000000 | bytes 20000000 | tf_op jit(solution)/shard_map/project_back/pallas_call | solution.py:42
  231.1 6.0 %outer_grads.7 = bf16[2,768,768]{2,1,0:T(8,128)(2,1)} custom-call(bf16[768,768]{1,0:T(8,128)(2,1)} %get-tuple-element.145.left, bf16[4,768,768]{2,1,0:T(8,128)(2,1)} %get-tuple-element.146.right), custom_call_target="tpu_custom_call" | custom-call | flops 1812000000 | bytes 6000000 | tf_op jit(solution)/shard_map/outer_grads/pallas_call | solution.py:42
  239.0 2.3 collective-permute-done.24
  242.9 6.0 %outer_grads.5 = bf16[2,768,768]{2,1,0:T(8,128)(2,1)} custom-call(bf16[768,768]{1,0:T(8,128)(2,1)} %get-tuple-element.143.left, bf16[4,768,768]{2,1,0:T(8,128)(2,1)} %get-tuple-element.144.right), custom_call_target="tpu_custom_call" | custom-call | flops 1812000000 | bytes 6000000 | tf_op jit(solution)/shard_map/outer_grads/pallas_call | solution.py:42
  250.6 6.0 %outer_grads.6 = bf16[2,768,768]{2,1,0:T(8,128)(2,1)} custom-call(bf16[768,768]{1,0:T(8,128)(2,1)} %get-tuple-element.145.left, bf16[4,768,768]{2,1,0:T(8,128)(2,1)} %get-tuple-element.146.right), custom_call_target="tpu_custom_call" | custom-call | flops 1812000000 | bytes 6000000 | tf_op jit(solution)/shard_map/outer_grads/pallas_call | solution.py:42
  256.9 2.6 collective-permute-start.27
  259.5 6.1 %outer_grads.4 = bf16[2,768,768]{2,1,0:T(8,128)(2,1)} custom-call(bf16[768,768]{1,0:T(8,128)(2,1)} %get-tuple-element.143.left, bf16[4,768,768]{2,1,0:T(8,128)(2,1)} %get-tuple-element.144.right), custom_call_target="tpu_custom_call" | custom-call | flops 1812000000 | bytes 6000000 | tf_op jit(solution)/shard_map/outer_grads/pallas_call | solution.py:42
  265.6 2.9 convert_element_type.268
  272.7 2.2 add_convert_fusion.1
  281.4 5.3 %collective-permute-done.36 = bf16[768,384]{1,0:T(8,128)(2,1)S(1)} collective-permute-done((bf16[768,384]{1,0:T(8,128)(2,1)S(1)}, bf16[768,384]{1,0:T(8,128)(2,1)S(1)}, u32[]{:S(2)}, u32[]{:S(2)}) %collective-permute-start.36) | collective-permute-done | bytes 589856 | tf_op jit(solution)/shard_map/ppermute | solution.py:592
  289.3 10.1 %collective-permute-done.29 = bf16[768,384]{1,0:T(8,128)(2,1)S(1)} collective-permute-done((bf16[768,384]{1,0:T(8,128)(2,1)S(1)}, bf16[768,384]{1,0:T(8,128)(2,1)S(1)}, u32[]{:S(2)}, u32[]{:S(2)}) %collective-permute-start.29) | collective-permute-done | bytes 589856 | tf_op jit(solution)/shard_map/ppermute | solution.py:592
  301.9 15.6 %collective-permute-done.39 = bf16[4,96,384]{2,1,0:T(8,128)(2,1)S(1)} collective-permute-done((bf16[4,96,384]{2,1,0:T(8,128)(2,1)S(1)}, bf16[4,96,384]{2,1,0:T(8,128)(2,1)S(1)}, u32[]{:S(2)}, u32[]{:S(2)}) %collective-permute-start.39) | collective-permute-done | bytes 294944 | tf_op jit(solution)/shard_map/ppermute | solution.py:592
  320.7 4.4 %collective-permute-done.30 = bf16[4,96,384]{2,1,0:T(8,128)(2,1)S(1)} collective-permute-done((bf16[4,96,384]{2,1,0:T(8,128)(2,1)S(1)}, bf16[4,96,384]{2,1,0:T(8,128)(2,1)S(1)}, u32[]{:S(2)}, u32[]{:S(2)}) %collective-permute-start.30) | collective-permute-done | bytes 294944 | tf_op jit(solution)/shard_map/ppermute | solution.py:592
  329.3 8.4 %collective-permute-done.33 = bf16[2,96,768]{2,1,0:T(8,128)(2,1)S(1)} collective-permute-done((bf16[2,96,768]{2,1,0:T(8,128)(2,1)S(1)}, bf16[2,96,768]{2,1,0:T(8,128)(2,1)S(1)}, u32[]{:S(2)}, u32[]{:S(2)}) %collective-permute-start.33) | collective-permute-done | bytes 294944 | tf_op jit(solution)/shard_map/ppermute | solution.py:592
  339.0 7.3 %collective-permute-done.21 = bf16[2,96,768]{2,1,0:T(8,128)(2,1)S(1)} collective-permute-done((bf16[2,96,768]{2,1,0:T(8,128)(2,1)S(1)}, bf16[2,96,768]{2,1,0:T(8,128)(2,1)S(1)}, u32[]{:S(2)}, u32[]{:S(2)}) %collective-permute-start.21) | collective-permute-done | bytes 294944 | tf_op jit(solution)/shard_map/ppermute | solution.py:592
  348.3 4.7 %collective-permute-done.22 = bf16[1,96,768]{2,1,0:T(8,128)(2,1)S(1)} collective-permute-done((bf16[1,96,768]{2,1,0:T(8,128)(2,1)S(1)}, bf16[1,96,768]{2,1,0:T(8,128)(2,1)S(1)}, u32[]{:S(2)}, u32[]{:S(2)}) %collective-permute-start.22) | collective-permute-done | bytes 147488 | tf_op jit(solution)/shard_map/ppermute | solution.py:592
  (224 shorter events, 80.3 us)
Async XLA Ops:
  1.5 37.0 %collective-permute-start.3 = (f32[1152]{0:T(1024)S(1)}, f32[1152]{0:T(1024)}, u32[]{:S(2)}, u32[]{:S(2)}) collective-permute-start(f32[1152]{0:T(1024)S(1)} %concatenate.39), channel_id=1, source_target_pairs={{0,1},{1,0},{2,3},{3,2},{4,5},{5,4},{6,7},{7,6},{8,9},{9,8},{10,11... | collective-permute-start | bytes 13832 | tf_op jit(solution)/shard_map/ppermute | solution.py:592
  3.3 71.0 %collective-permute-start.5 = (bf16[768,768]{1,0:T(8,128)(2,1)S(1)}, bf16[768,768]{1,0:T(8,128)(2,1)}, u32[]{:S(2)}, u32[]{:S(2)}) collective-permute-start(bf16[768,768]{1,0:T(8,128)(2,1)S(1)} %pad_maximum_fusion.a_ref), channel_id=1, source_target_pairs={{0,1},{1,0},{2,3},{3,2},{4,5},{5,4},{6,7},{7,6},{8,9},{9,8},{10,11... | collective-permute-start | bytes 3538952 | tf_op jit(solution)/shard_map/ppermute | solution.py:592
  3.5 22.3 %collective-permute-start = (bf16[384,768]{1,0:T(8,128)(2,1)S(1)}, bf16[384,768]{1,0:T(8,128)(2,1)}, u32[]{:S(2)}, u32[]{:S(2)}) collective-permute-start(bf16[384,768]{1,0:T(8,128)(2,1)S(1)} %constant_dynamic-slice_fusion.28), channel_id=1, source_target_pairs={{0,2},{1,3},{2,0},{3,1},{4,6},{5,7},{6,4},{7,5},{8,10},{9,11},{10,... | collective-permute-start | bytes 1769480 | tf_op jit(solution)/shard_map/ppermute | solution.py:592
  8.4 35.3 %collective-permute-start.9 = (bf16[384,768]{1,0:T(8,128)(2,1)}, bf16[384,768]{1,0:T(8,128)(2,1)S(1)}, u32[]{:S(2)}, u32[]{:S(2)}) collective-permute-start(bf16[384,768]{1,0:T(8,128)(2,1)} %constant_dynamic-slice_fusion.26), channel_id=1, source_target_pairs={{0,2},{1,3},{2,0},{3,1},{4,6},{5,7},{6,4},{7,5},{8,10},{9,11},{10,... | collective-permute-start | bytes 1769480 | tf_op jit(solution)/shard_map/ppermute | solution.py:592
  9.3 36.0 %collective-permute-start.6 = (bf16[384,768]{1,0:T(8,128)(2,1)}, bf16[384,768]{1,0:T(8,128)(2,1)S(1)}, u32[]{:S(2)}, u32[]{:S(2)}) collective-permute-start(bf16[384,768]{1,0:T(8,128)(2,1)} %constant_dynamic-slice_fusion.27), channel_id=1, source_target_pairs={{0,2},{1,3},{2,0},{3,1},{4,6},{5,7},{6,4},{7,5},{8,10},{9,11},{10,... | collective-permute-start | bytes 1769480 | tf_op jit(solution)/shard_map/ppermute | solution.py:592
  25.9 21.2 %collective-permute-start.1 = (bf16[384,768]{1,0:T(8,128)(2,1)}, bf16[384,768]{1,0:T(8,128)(2,1)}, u32[]{:S(2)}, u32[]{:S(2)}) collective-permute-start(bf16[384,768]{1,0:T(8,128)(2,1)} %collective-permute-done), channel_id=1, source_target_pairs={{0,4},{1,5},{2,6},{3,7},{4,0},{5,1},{6,2},{7,3},{8,12},{9,13},{10,... | collective-permute-start | bytes 1769480 | tf_op jit(solution)/shard_map/ppermute | solution.py:592
  38.4 75.9 %collective-permute-start.12 = (bf16[768,768]{1,0:T(8,128)(2,1)}, bf16[768,768]{1,0:T(8,128)(2,1)}, u32[]{:S(2)}, u32[]{:S(2)}) collective-permute-start(bf16[768,768]{1,0:T(8,128)(2,1)} %ua.1), channel_id=1, source_target_pairs={{0,1},{1,0},{2,3},{3,2},{4,5},{5,4},{6,7},{7,6},{8,9},{9,8},{10,11... | collective-permute-start | bytes 3538952 | tf_op jit(solution)/shard_map/ppermute | solution.py:592
  45.3 16.3 %collective-permute-start.10 = (bf16[384,768]{1,0:T(8,128)(2,1)S(1)}, bf16[384,768]{1,0:T(8,128)(2,1)S(1)}, u32[]{:S(2)}, u32[]{:S(2)}) collective-permute-start(bf16[384,768]{1,0:T(8,128)(2,1)S(1)} %collective-permute-done.9), channel_id=1, source_target_pairs={{0,4},{1,5},{2,6},{3,7},{4,0},{5,1},{6,2},{7,3},{8,12},{9,13},{10,... | collective-permute-start | bytes 1769480 | tf_op jit(solution)/shard_map/ppermute | solution.py:592
  47.1 25.6 %collective-permute-start.7 = (bf16[384,768]{1,0:T(8,128)(2,1)S(1)}, bf16[384,768]{1,0:T(8,128)(2,1)S(1)}, u32[]{:S(2)}, u32[]{:S(2)}) collective-permute-start(bf16[384,768]{1,0:T(8,128)(2,1)S(1)} %collective-permute-done.6), channel_id=1, source_target_pairs={{0,4},{1,5},{2,6},{3,7},{4,0},{5,1},{6,2},{7,3},{8,12},{9,13},{10,... | collective-permute-start | bytes 1769480 | tf_op jit(solution)/shard_map/ppermute | solution.py:592
  50.4 46.3 %collective-permute-start.2 = (bf16[768,768]{1,0:T(8,128)(2,1)}, bf16[768,768]{1,0:T(8,128)(2,1)}, u32[]{:S(2)}, u32[]{:S(2)}) collective-permute-start(bf16[768,768]{1,0:T(8,128)(2,1)} %maximum_select_fusion.a_ref), channel_id=1, source_target_pairs={{0,1},{1,0},{2,3},{3,2},{4,5},{5,4},{6,7},{7,6},{8,9},{9,8},{10,11... | collective-permute-start | bytes 3538952 | tf_op jit(solution)/shard_map/ppermute | solution.py:592
  61.6 52.7 %collective-permute-start.13 = (bf16[768,768]{1,0:T(8,128)(2,1)}, bf16[768,768]{1,0:T(8,128)(2,1)}, u32[]{:S(2)}, u32[]{:S(2)}) collective-permute-start(bf16[768,768]{1,0:T(8,128)(2,1)} %na.1), channel_id=1, source_target_pairs={{0,1},{1,0},{2,3},{3,2},{4,5},{5,4},{6,7},{7,6},{8,9},{9,8},{10,11... | collective-permute-start | bytes 3538952 | tf_op jit(solution)/shard_map/ppermute | solution.py:592
  72.7 53.3 %collective-permute-start.11 = (bf16[768,768]{1,0:T(8,128)(2,1)S(1)}, bf16[768,768]{1,0:T(8,128)(2,1)}, u32[]{:S(2)}, u32[]{:S(2)}) collective-permute-start(bf16[768,768]{1,0:T(8,128)(2,1)S(1)} %maximum_select_fusion.2.na), channel_id=1, source_target_pairs={{0,1},{1,0},{2,3},{3,2},{4,5},{5,4},{6,7},{7,6},{8,9},{9,8},{10,11... | collective-permute-start | bytes 3538952 | tf_op jit(solution)/shard_map/ppermute | solution.py:592
  74.4 51.6 %collective-permute-start.8 = (bf16[768,768]{1,0:T(8,128)(2,1)S(1)}, bf16[768,768]{1,0:T(8,128)(2,1)S(1)}, u32[]{:S(2)}, u32[]{:S(2)}) collective-permute-start(bf16[768,768]{1,0:T(8,128)(2,1)S(1)} %maximum_select_fusion.1.ua), channel_id=1, source_target_pairs={{0,1},{1,0},{2,3},{3,2},{4,5},{5,4},{6,7},{7,6},{8,9},{9,8},{10,11... | collective-permute-start | bytes 3538952 | tf_op jit(solution)/shard_map/ppermute | solution.py:592
  237.2 32.6 %collective-permute-start.35 = (bf16[2,768,768]{2,1,0:T(8,128)(2,1)}, bf16[2,768,768]{2,1,0:T(8,128)(2,1)S(1)}, u32[]{:S(2)}, u32[]{:S(2)}) collective-permute-start(bf16[2,768,768]{2,1,0:T(8,128)(2,1)} %outer_grads.7), channel_id=1, source_target_pairs={{0,1},{1,0},{2,3},{3,2},{4,5},{5,4},{6,7},{7,6},{8,9},{9,8},{10,11... | collective-permute-start | bytes 7077896 | tf_op jit(solution)/shard_map/ppermute | solution.py:592
  248.9 23.8 %collective-permute-start.28 = (bf16[2,768,768]{2,1,0:T(8,128)(2,1)}, bf16[2,768,768]{2,1,0:T(8,128)(2,1)}, u32[]{:S(2)}, u32[]{:S(2)}) collective-permute-start(bf16[2,768,768]{2,1,0:T(8,128)(2,1)} %outer_grads.5), channel_id=1, source_target_pairs={{0,1},{1,0},{2,3},{3,2},{4,5},{5,4},{6,7},{7,6},{8,9},{9,8},{10,11... | collective-permute-start | bytes 7077896 | tf_op jit(solution)/shard_map/ppermute | solution.py:592
  256.6 20.7 %collective-permute-start.16 = (bf16[2,768,768]{2,1,0:T(8,128)(2,1)}, bf16[2,768,768]{2,1,0:T(8,128)(2,1)}, u32[]{:S(2)}, u32[]{:S(2)}) collective-permute-start(bf16[2,768,768]{2,1,0:T(8,128)(2,1)} %get-tuple-element.137), channel_id=1, source_target_pairs={{0,1},{1,0},{2,3},{3,2},{4,5},{5,4},{6,7},{7,6},{8,9},{9,8},{10,11... | collective-permute-start | bytes 7077896 | tf_op jit(solution)/shard_map/ppermute | solution.py:592
  256.9 11.7 %collective-permute-start.27 = (f32[1,432]{1,0:T(1,128)S(1)}, f32[1,432]{1,0:T(1,128)S(1)}, u32[]{:S(2)}, u32[]{:S(2)}) collective-permute-start(f32[1,432]{1,0:T(1,128)S(1)} %constant_dynamic-slice_fusion.2), channel_id=1, source_target_pairs={{0,16},{1,17},{2,18},{3,19},{4,20},{5,21},{6,22},{7,23},{8,24},{9,... | collective-permute-start | bytes 5192 | tf_op jit(solution)/shard_map/ppermute | solution.py:592
  270.5 16.3 %collective-permute-start.36 = (bf16[768,384]{1,0:T(8,128)(2,1)S(1)}, bf16[768,384]{1,0:T(8,128)(2,1)S(1)}, u32[]{:S(2)}, u32[]{:S(2)}) collective-permute-start(bf16[768,384]{1,0:T(8,128)(2,1)S(1)} %slice_bitcast_fusion), channel_id=1, source_target_pairs={{0,2},{1,3},{2,0},{3,1},{4,6},{5,7},{6,4},{7,5},{8,10},{9,11},{10,... | collective-permute-start | bytes 1769480 | tf_op jit(solution)/shard_map/ppermute | solution.py:592
  272.1 16.3 %collective-permute-start.38 = (bf16[2,4,96,384]{3,2,1,0:T(8,128)(2,1)S(1)}, bf16[2,4,96,384]{3,2,1,0:T(8,128)(2,1)S(1)}, u32[]{:S(2)}, u32[]{:S(2)}) collective-permute-start(bf16[2,4,96,384]{3,2,1,0:T(8,128)(2,1)S(1)} %dynamic-slice_bitcast_fusion), channel_id=1, source_target_pairs={{0,4},{1,5},{2,6},{3,7},{4,0},{5,1},{6,2},{7,3},{8,12},{9,13},{10,... | collective-permute-start | bytes 1769480 | tf_op jit(solution)/shard_map/ppermute | solution.py:592
  275.1 24.3 %collective-permute-start.29 = (bf16[768,384]{1,0:T(8,128)(2,1)S(1)}, bf16[768,384]{1,0:T(8,128)(2,1)S(1)}, u32[]{:S(2)}, u32[]{:S(2)}) collective-permute-start(bf16[768,384]{1,0:T(8,128)(2,1)S(1)} %slice_bitcast_fusion.2), channel_id=1, source_target_pairs={{0,2},{1,3},{2,0},{3,1},{4,6},{5,7},{6,4},{7,5},{8,10},{9,11},{10,... | collective-permute-start | bytes 1769480 | tf_op jit(solution)/shard_map/ppermute | solution.py:592
  276.0 25.1 %collective-permute-start.31 = (bf16[2,4,96,384]{3,2,1,0:T(8,128)(2,1)S(1)}, bf16[2,4,96,384]{3,2,1,0:T(8,128)(2,1)S(1)}, u32[]{:S(2)}, u32[]{:S(2)}) collective-permute-start(bf16[2,4,96,384]{3,2,1,0:T(8,128)(2,1)S(1)} %dynamic-slice_bitcast_fusion.1), channel_id=1, source_target_pairs={{0,4},{1,5},{2,6},{3,7},{4,0},{5,1},{6,2},{7,3},{8,12},{9,13},{10,... | collective-permute-start | bytes 1769480 | tf_op jit(solution)/shard_map/ppermute | solution.py:592
  279.8 46.4 %collective-permute-start.17 = (bf16[768,384]{1,0:T(8,128)(2,1)S(1)}, bf16[768,384]{1,0:T(8,128)(2,1)S(1)}, u32[]{:S(2)}, u32[]{:S(2)}) collective-permute-start(bf16[768,384]{1,0:T(8,128)(2,1)S(1)} %slice_bitcast_fusion.4), channel_id=1, source_target_pairs={{0,2},{1,3},{2,0},{3,1},{4,6},{5,7},{6,4},{7,5},{8,10},{9,11},{10,... | collective-permute-start | bytes 1769480 | tf_op jit(solution)/shard_map/ppermute | solution.py:592
  286.8 40.2 %collective-permute-start.19 = (bf16[2,4,96,384]{3,2,1,0:T(8,128)(2,1)S(1)}, bf16[2,4,96,384]{3,2,1,0:T(8,128)(2,1)S(1)}, u32[]{:S(2)}, u32[]{:S(2)}) collective-permute-start(bf16[2,4,96,384]{3,2,1,0:T(8,128)(2,1)S(1)} %dynamic-slice_bitcast_fusion.2), channel_id=1, source_target_pairs={{0,4},{1,5},{2,6},{3,7},{4,0},{5,1},{6,2},{7,3},{8,12},{9,13},{10,... | collective-permute-start | bytes 1769480 | tf_op jit(solution)/shard_map/ppermute | solution.py:592
  288.4 31.6 %collective-permute-start.37 = (bf16[4,96,384]{2,1,0:T(8,128)(2,1)S(1)}, bf16[4,96,384]{2,1,0:T(8,128)(2,1)S(1)}, u32[]{:S(2)}, u32[]{:S(2)}) collective-permute-start(bf16[4,96,384]{2,1,0:T(8,128)(2,1)S(1)} %dynamic-slice_bitcast_fusion.4), channel_id=1, source_target_pairs={{0,4},{1,5},{2,6},{3,7},{4,0},{5,1},{6,2},{7,3},{8,12},{9,13},{10,... | collective-permute-start | bytes 884744 | tf_op jit(solution)/shard_map/ppermute | solution.py:592
  299.4 18.0 %collective-permute-start.39 = (bf16[4,96,384]{2,1,0:T(8,128)(2,1)S(1)}, bf16[4,96,384]{2,1,0:T(8,128)(2,1)S(1)}, u32[]{:S(2)}, u32[]{:S(2)}) collective-permute-start(bf16[4,96,384]{2,1,0:T(8,128)(2,1)S(1)} %slice_bitcast_fusion.6), channel_id=1, source_target_pairs={{0,2},{1,3},{2,0},{3,1},{4,6},{5,7},{6,4},{7,5},{8,10},{9,11},{10,... | collective-permute-start | bytes 884744 | tf_op jit(solution)/shard_map/ppermute | solution.py:592
  301.1 24.0 %collective-permute-start.30 = (bf16[4,96,384]{2,1,0:T(8,128)(2,1)S(1)}, bf16[4,96,384]{2,1,0:T(8,128)(2,1)S(1)}, u32[]{:S(2)}, u32[]{:S(2)}) collective-permute-start(bf16[4,96,384]{2,1,0:T(8,128)(2,1)S(1)} %dynamic-slice_bitcast_fusion.6), channel_id=1, source_target_pairs={{0,4},{1,5},{2,6},{3,7},{4,0},{5,1},{6,2},{7,3},{8,12},{9,13},{10,... | collective-permute-start | bytes 884744 | tf_op jit(solution)/shard_map/ppermute | solution.py:592
  320.2 8.5 %collective-permute-start.40 = (bf16[2,96,768]{2,1,0:T(8,128)(2,1)S(1)}, bf16[2,96,768]{2,1,0:T(8,128)(2,1)S(1)}, u32[]{:S(2)}, u32[]{:S(2)}) collective-permute-start(bf16[2,96,768]{2,1,0:T(8,128)(2,1)S(1)} %dynamic-slice_bitcast_fusion.3), channel_id=1, source_target_pairs={{0,8},{1,9},{2,10},{3,11},{4,12},{5,13},{6,14},{7,15},{8,0},{9,1},... | collective-permute-start | bytes 884744 | tf_op jit(solution)/shard_map/ppermute | solution.py:592
  325.7 11.9 %collective-permute-start.33 = (bf16[2,96,768]{2,1,0:T(8,128)(2,1)S(1)}, bf16[2,96,768]{2,1,0:T(8,128)(2,1)S(1)}, u32[]{:S(2)}, u32[]{:S(2)}) collective-permute-start(bf16[2,96,768]{2,1,0:T(8,128)(2,1)S(1)} %dynamic-slice_bitcast_fusion.5), channel_id=1, source_target_pairs={{0,8},{1,9},{2,10},{3,11},{4,12},{5,13},{6,14},{7,15},{8,0},{9,1},... | collective-permute-start | bytes 884744 | tf_op jit(solution)/shard_map/ppermute | solution.py:592
  326.4 11.3 %collective-permute-start.18 = (bf16[4,96,384]{2,1,0:T(8,128)(2,1)S(1)}, bf16[4,96,384]{2,1,0:T(8,128)(2,1)S(1)}, u32[]{:S(2)}, u32[]{:S(2)}) collective-permute-start(bf16[4,96,384]{2,1,0:T(8,128)(2,1)S(1)} %dynamic-slice_bitcast_fusion.8), channel_id=1, source_target_pairs={{0,4},{1,5},{2,6},{3,7},{4,0},{5,1},{6,2},{7,3},{8,12},{9,13},{10,... | collective-permute-start | bytes 884744 | tf_op jit(solution)/shard_map/ppermute | solution.py:592
  327.2 10.6 %collective-permute-start.20 = (bf16[4,96,384]{2,1,0:T(8,128)(2,1)S(1)}, bf16[4,96,384]{2,1,0:T(8,128)(2,1)S(1)}, u32[]{:S(2)}, u32[]{:S(2)}) collective-permute-start(bf16[4,96,384]{2,1,0:T(8,128)(2,1)S(1)} %slice_bitcast_fusion.10), channel_id=1, source_target_pairs={{0,2},{1,3},{2,0},{3,1},{4,6},{5,7},{6,4},{7,5},{8,10},{9,11},{10,... | collective-permute-start | bytes 884744 | tf_op jit(solution)/shard_map/ppermute | solution.py:592
  328.9 9.3 %collective-permute-start.41 = (bf16[1,96,768]{2,1,0:T(8,128)(2,1)S(1)}, bf16[1,96,768]{2,1,0:T(8,128)(2,1)S(1)}, u32[]{:S(2)}, u32[]{:S(2)}) collective-permute-start(bf16[1,96,768]{2,1,0:T(8,128)(2,1)S(1)} %constant_dynamic-slice_fusion), channel_id=1, source_target_pairs={{0,16},{1,17},{2,18},{3,19},{4,20},{5,21},{6,22},{7,23},{8,24},{9,... | collective-permute-start | bytes 442376 | tf_op jit(solution)/shard_map/ppermute | solution.py:592
  338.1 9.5 %collective-permute-start.34 = (bf16[1,96,768]{2,1,0:T(8,128)(2,1)S(1)}, bf16[1,96,768]{2,1,0:T(8,128)(2,1)S(1)}, u32[]{:S(2)}, u32[]{:S(2)}) collective-permute-start(bf16[1,96,768]{2,1,0:T(8,128)(2,1)S(1)} %constant_dynamic-slice_fusion.1), channel_id=1, source_target_pairs={{0,16},{1,17},{2,18},{3,19},{4,20},{5,21},{6,22},{7,23},{8,24},{9,... | collective-permute-start | bytes 442376 | tf_op jit(solution)/shard_map/ppermute | solution.py:592
  (26 other events, 177.4 us)
